TPU v7x, 32 devices: a whole 2x2x4 slice. The times are simulated.
32 devices in a mesh: dp: 4 (over y, x), ctx: 8 (over z, core).
Axes of the slice: x: 2, y: 2, z: 4, core: 2. Of those that a mesh axis runs over, the one named last changes fastest.
Arguments:
- inputs: bfloat16 [4, 2048, 2048], P('dp', 'ctx'), may hold values from -6 to 6
- targets: bfloat16 [4, 2048, 2048], P('dp', 'ctx'), may hold values from -6 to 6
- valid: int32 [4, 2048], P('dp', 'ctx'), may hold values from 0 to 1, as said below
- positions: int32 [4, 2048], P('dp', 'ctx'), may hold values from 0 to 3070, as said below
- ln1_gain: bfloat16 [2048], P(('dp', 'ctx')), may hold values from 0.5 to 1.5
- w_query: bfloat16 [2048, 2048], P(('dp', 'ctx')), may hold values from -0.125 to 0.125
- w_key: bfloat16 [2048, 1024], P(('dp', 'ctx')), may hold values from -0.125 to 0.125
- w_value: bfloat16 [2048, 1024], P(('dp', 'ctx')), may hold values from -0.125 to 0.125
- w_gatelogit: bfloat16 [2048, 16], P(('dp', 'ctx')), may hold values from -0.25 to 0.25
- q_gain: bfloat16 [128], P(('dp', 'ctx')), may hold values from 0.5 to 1.5
- k_gain: bfloat16 [128], P(('dp', 'ctx')), may hold values from 0.5 to 1.5
- w_output: bfloat16 [2048, 2048], P(None, ('dp', 'ctx')), may hold values from -6 to 6
- ln2_gain: bfloat16 [2048], P(('dp', 'ctx')), may hold values from 0.25 to 2.5
- w_gate: bfloat16 [2048, 6144], P(('dp', 'ctx')), may hold values from -0.125 to 0.125
- w_up: bfloat16 [2048, 6144], P(('dp', 'ctx')), may hold values from -0.125 to 0.125
- w_down: bfloat16 [6144, 2048], P(None, ('dp', 'ctx')), may hold values from -0.078125 to 0.078125
Outputs:
- output: bfloat16 [4, 2048, 2048], P('dp', 'ctx')
- loss: float32 [], replicated
- grad_inputs: float32 [4, 2048, 2048], P('dp', 'ctx')
- grad_ln1_gain: float32 [2048], P(('dp', 'ctx'))
- grad_w_query: float32 [2048, 2048], P(('dp', 'ctx'))
- grad_w_key: float32 [2048, 1024], P(('dp', 'ctx'))
- grad_w_value: float32 [2048, 1024], P(('dp', 'ctx'))
- grad_w_gatelogit: float32 [2048, 16], P(('dp', 'ctx'))
- grad_q_gain: float32 [128], P(('dp', 'ctx'))
- grad_k_gain: float32 [128], P(('dp', 'ctx'))
- grad_w_output: float32 [2048, 2048], P(None, ('dp', 'ctx'))
- grad_ln2_gain: float32 [2048], P(('dp', 'ctx'))
- grad_w_gate: float32 [2048, 6144], P(('dp', 'ctx'))
- grad_w_up: float32 [2048, 6144], P(('dp', 'ctx'))
- grad_w_down: float32 [6144, 2048], P(None, ('dp', 'ctx'))
Inputs may be any that keep to these rules, and one draw needn't show every extreme that they name: The first token of every sequence has valid = 1. Along each sequence positions start at 0 and rise by 1 or 2 from one token to the next, by 2 at exactly (2047) // 2 of the steps.
All inputs are finite; a program needn't handle non-finite values.
Results may differ from a plain program's by a relative error of at most 0.017.
Values may be sent and summed in bfloat16 or wider, within the bound.
A program may use at most 512 MiB of HBM per device.

v0:
```python
import math

import jax
import jax.numpy as jnp
from jax import lax
from jax.sharding import PartitionSpec as P

H = 16
KV = 8
HD = 128


EPSILON = 1e-06
ROPE_BASE = 1000000.0
MASKED = -1e30


def normalize(values):
    return values * lax.rsqrt(jnp.mean(values * values, axis=-1, keepdims=True) + EPSILON)


def norm_back(grad, values):
    factor = lax.rsqrt(jnp.mean(values * values, axis=-1, keepdims=True) + EPSILON)
    unit = values * factor
    return factor * (grad - unit * jnp.mean(grad * unit, axis=-1, keepdims=True))


def rope_tables(places):
    half_width = HD // 2
    frequency = ROPE_BASE ** (-(jnp.arange(half_width, dtype=jnp.float32) * 2.0 / HD))
    angles = places.astype(jnp.float32)[:, None] * frequency[None, :]
    cosine = jnp.concatenate([jnp.cos(angles), jnp.cos(angles)], axis=-1)
    sine = jnp.concatenate([jnp.sin(angles), jnp.sin(angles)], axis=-1)
    return (cosine, sine)


def rotate(values):
    half_width = values.shape[-1] // 2
    return jnp.concatenate([-values[..., half_width:], values[..., :half_width]], axis=-1)


def rotate_back(values):
    half_width = values.shape[-1] // 2
    return jnp.concatenate([values[..., half_width:], -values[..., :half_width]], axis=-1)


def apply_rope(heads, cosine, sine):
    return heads * cosine[:, None, :] + rotate(heads) * sine[:, None, :]


def rope_back(grad, cosine, sine):
    return grad * cosine[:, None, :] + rotate_back(grad * sine[:, None, :])


def contract_rows(left, right):
    return lax.dot_general(
        left, right, (((0,), (0,)), ((), ())), preferred_element_type=jnp.float32
    )


def contract_cols(left, right):
    return lax.dot_general(
        left, right, (((1,), (1,)), ((), ())), preferred_element_type=jnp.float32
    )


def block_scores(queries, keys_all, values_all, first_row, step_index, key_block):
    place = step_index * key_block
    keys_here = lax.dynamic_slice_in_dim(keys_all, place, key_block, 0)
    values_here = lax.dynamic_slice_in_dim(values_all, place, key_block, 0)
    scores = jnp.einsum(
        "tkgd,skd->kgts", queries, keys_here, preferred_element_type=jnp.float32
    ) * queries.shape[-1] ** (-0.5)
    key_rows = place + lax.iota(jnp.int32, key_block)
    query_rows = first_row + lax.iota(jnp.int32, queries.shape[0])
    causal = key_rows[None, :] <= query_rows[:, None]
    return (scores, causal, keys_here, values_here)


def attend(queries, keys_all, values_all, first_row, key_block):
    rows_here = queries.shape[0]
    blocks_needed = (first_row + rows_here + key_block - 1) // key_block
    score_shape = (queries.shape[1], queries.shape[2], rows_here)

    def statistics(step_index, carried):
        running_max, running_sum = carried
        scores, causal, keys_here, values_here = block_scores(
            queries, keys_all, values_all, first_row, step_index, key_block
        )
        scores = jnp.where(causal, scores, MASKED)
        new_max = jnp.maximum(running_max, jnp.max(scores, axis=-1))
        weights_here = jnp.where(causal, jnp.exp(scores - new_max[..., None]), 0.0)
        return (
            new_max,
            running_sum * jnp.exp(running_max - new_max) + jnp.sum(weights_here, axis=-1),
        )

    start_state = (jnp.full(score_shape, MASKED, jnp.float32), jnp.zeros(score_shape, jnp.float32))
    running_max, running_sum = lax.fori_loop(0, blocks_needed, statistics, start_state)
    log_total = running_max + jnp.log(running_sum)

    def weigh(step_index, weighted):
        scores, causal, keys_here, values_here = block_scores(
            queries, keys_all, values_all, first_row, step_index, key_block
        )
        probs = jnp.where(causal, jnp.exp(scores - log_total[..., None]), 0.0).astype(jnp.bfloat16)
        return weighted + jnp.einsum(
            "kgts,skd->tkgd", probs, values_here, preferred_element_type=jnp.float32
        )

    weighted = lax.fori_loop(0, blocks_needed, weigh, jnp.zeros(queries.shape, jnp.float32))
    return (weighted, log_total)


def attend_back(
    queries, keys_all, values_all, first_row, key_block, log_total, d_attended, row_dot
):
    rows_here = queries.shape[0]
    blocks_needed = (first_row + rows_here + key_block - 1) // key_block
    score_scale = queries.shape[-1] ** (-0.5)

    def accumulate(step_index, carried):
        d_queries, d_keys_all, d_values_all = carried
        scores, causal, keys_here, values_here = block_scores(
            queries, keys_all, values_all, first_row, step_index, key_block
        )
        probs = jnp.where(causal, jnp.exp(scores - log_total[..., None]), 0.0)
        d_probs = jnp.einsum(
            "tkgd,skd->kgts", d_attended, values_here, preferred_element_type=jnp.float32
        )
        d_scores = (probs * (d_probs - row_dot[..., None])).astype(jnp.bfloat16)
        d_queries = (
            d_queries
            + jnp.einsum("kgts,skd->tkgd", d_scores, keys_here, preferred_element_type=jnp.float32)
            * score_scale
        )
        d_keys_here = (
            jnp.einsum("kgts,tkgd->skd", d_scores, queries, preferred_element_type=jnp.float32)
            * score_scale
        )
        d_values_here = jnp.einsum(
            "kgts,tkgd->skd",
            probs.astype(jnp.bfloat16),
            d_attended,
            preferred_element_type=jnp.float32,
        )
        place = step_index * key_block
        d_keys_all = lax.dynamic_update_slice_in_dim(d_keys_all, d_keys_here, place, 0)
        d_values_all = lax.dynamic_update_slice_in_dim(d_values_all, d_values_here, place, 0)
        return (d_queries, d_keys_all, d_values_all)

    start_state = (
        jnp.zeros(queries.shape, jnp.float32),
        jnp.zeros(keys_all.shape, jnp.float32),
        jnp.zeros(values_all.shape, jnp.float32),
    )
    return lax.fori_loop(0, blocks_needed, accumulate, start_state)


def on_device(
    inputs,
    targets,
    valid,
    positions,
    ln1_gain,
    w_query,
    w_key,
    w_value,
    w_gatelogit,
    q_gain,
    k_gain,
    w_output,
    ln2_gain,
    w_gate,
    w_up,
    w_down,
):
    attn_full = (
        lax.all_gather(ln1_gain, ("dp", "ctx"), axis=0, tiled=True),
        lax.all_gather(w_query, ("dp", "ctx"), axis=0, tiled=True),
        lax.all_gather(w_key, ("dp", "ctx"), axis=0, tiled=True),
        lax.all_gather(w_value, ("dp", "ctx"), axis=0, tiled=True),
        lax.all_gather(w_gatelogit, ("dp", "ctx"), axis=0, tiled=True),
        lax.all_gather(q_gain, ("dp", "ctx"), axis=0, tiled=True),
        lax.all_gather(k_gain, ("dp", "ctx"), axis=0, tiled=True),
        lax.all_gather(w_output, ("dp", "ctx"), axis=1, tiled=True),
    )
    mlp_full = (
        lax.all_gather(ln2_gain, ("dp", "ctx"), axis=0, tiled=True),
        lax.all_gather(w_gate, ("dp", "ctx"), axis=0, tiled=True),
        lax.all_gather(w_up, ("dp", "ctx"), axis=0, tiled=True),
        lax.all_gather(w_down, ("dp", "ctx"), axis=1, tiled=True),
    )
    gain_one = attn_full[0].astype(jnp.float32)
    gain_q = attn_full[5].astype(jnp.float32)
    gain_k = attn_full[6].astype(jnp.float32)
    gain_two = mlp_full[0].astype(jnp.float32)
    hidden_in = inputs[0].astype(jnp.float32)
    rows_here = hidden_in.shape[0]
    groups = H // KV
    first_row = lax.axis_index("ctx") * rows_here
    cosine, sine = rope_tables(positions[0])
    unit_in = normalize(hidden_in)
    normed_in = (unit_in * gain_one).astype(jnp.bfloat16)
    query_raw = jnp.dot(normed_in, attn_full[1], preferred_element_type=jnp.float32)
    key_raw = jnp.dot(normed_in, attn_full[2], preferred_element_type=jnp.float32)
    value_raw = jnp.dot(normed_in, attn_full[3], preferred_element_type=jnp.float32)
    gate_logit = jnp.dot(normed_in, attn_full[4], preferred_element_type=jnp.float32)
    query_heads = query_raw.reshape(rows_here, H, HD)
    key_heads = key_raw.reshape(rows_here, KV, HD)
    unit_query = normalize(query_heads)
    unit_key = normalize(key_heads)
    queries = (
        apply_rope(unit_query * gain_q, cosine, sine)
        .astype(jnp.bfloat16)
        .reshape(rows_here, KV, groups, HD)
    )
    keys_own = apply_rope(unit_key * gain_k, cosine, sine).astype(jnp.bfloat16)
    values_own = value_raw.reshape(rows_here, KV, HD).astype(jnp.bfloat16)
    keys_all, values_all = (
        lax.all_gather(keys_own, "ctx", axis=0, tiled=True),
        lax.all_gather(values_own, "ctx", axis=0, tiled=True),
    )
    key_block = math.gcd(keys_all.shape[0], 512)
    attended, log_total = attend(queries, keys_all, values_all, first_row, key_block)
    gate_open = jax.nn.sigmoid(gate_logit)
    attended_heads = attended.reshape(rows_here, H, HD)
    gated = (attended_heads * gate_open[:, :, None]).reshape(rows_here, H * HD).astype(jnp.bfloat16)
    middle = hidden_in + jnp.dot(gated, attn_full[7], preferred_element_type=jnp.float32)
    unit_mid = normalize(middle)
    normed_mid = (unit_mid * gain_two).astype(jnp.bfloat16)
    gate_pre = jnp.dot(normed_mid, mlp_full[1], preferred_element_type=jnp.float32)
    up_proj = jnp.dot(normed_mid, mlp_full[2], preferred_element_type=jnp.float32)
    sigmoid_gate = jax.nn.sigmoid(gate_pre)
    activated = (gate_pre * sigmoid_gate * up_proj).astype(jnp.bfloat16)
    result = middle + jnp.dot(activated, mlp_full[3], preferred_element_type=jnp.float32)
    teacher = targets[0].astype(jnp.float32)
    weight_rows = valid[0].astype(jnp.float32)
    difference = result - teacher
    error_local = jnp.sum(weight_rows * jnp.mean(difference * difference, axis=-1))
    error_total, valid_count = lax.psum((error_local, jnp.sum(weight_rows)), ("dp", "ctx"))
    loss = error_total / valid_count
    tokens_all = lax.axis_size("dp") * lax.axis_size("ctx") * rows_here
    d_result = weight_rows[:, None] * difference * (tokens_all / valid_count)
    attn_back = (
        lax.all_gather(ln1_gain, ("dp", "ctx"), axis=0, tiled=True),
        lax.all_gather(w_query, ("dp", "ctx"), axis=0, tiled=True),
        lax.all_gather(w_key, ("dp", "ctx"), axis=0, tiled=True),
        lax.all_gather(w_value, ("dp", "ctx"), axis=0, tiled=True),
        lax.all_gather(w_gatelogit, ("dp", "ctx"), axis=0, tiled=True),
        lax.all_gather(q_gain, ("dp", "ctx"), axis=0, tiled=True),
        lax.all_gather(k_gain, ("dp", "ctx"), axis=0, tiled=True),
        lax.all_gather(w_output, ("dp", "ctx"), axis=1, tiled=True),
    )
    mlp_back = (
        lax.all_gather(ln2_gain, ("dp", "ctx"), axis=0, tiled=True),
        lax.all_gather(w_gate, ("dp", "ctx"), axis=0, tiled=True),
        lax.all_gather(w_up, ("dp", "ctx"), axis=0, tiled=True),
        lax.all_gather(w_down, ("dp", "ctx"), axis=1, tiled=True),
    )
    d_branch = d_result.astype(jnp.bfloat16)
    d_activated = contract_cols(d_branch, mlp_back[3])
    grad_down_full = contract_rows(activated, d_branch)
    d_gate = (
        d_activated * up_proj * sigmoid_gate * (1.0 + gate_pre * (1.0 - sigmoid_gate))
    ).astype(jnp.bfloat16)
    d_up = (d_activated * gate_pre * sigmoid_gate).astype(jnp.bfloat16)
    gate_up_share = lax.psum_scatter(
        jnp.concatenate(
            [contract_rows(normed_mid, d_gate), contract_rows(normed_mid, d_up)], axis=1
        ),
        ("dp", "ctx"),
        scatter_dimension=0,
        tiled=True,
    )
    d_normed_mid = contract_cols(d_gate, mlp_back[1]) + contract_cols(d_up, mlp_back[2])
    grad_gain_two = jnp.sum(d_normed_mid * unit_mid, axis=0)
    d_middle = d_result + norm_back(d_normed_mid * mlp_back[0].astype(jnp.float32), middle)
    d_attn = d_middle.astype(jnp.bfloat16)
    d_gated = contract_cols(d_attn, attn_back[7]).reshape(rows_here, H, HD)
    grad_out_full = contract_rows(gated, d_attn)
    d_attended = (
        (d_gated * gate_open[:, :, None]).astype(jnp.bfloat16).reshape(rows_here, KV, groups, HD)
    )
    d_gate_logit = (
        jnp.sum(d_gated * attended_heads, axis=-1) * gate_open * (1.0 - gate_open)
    ).astype(jnp.bfloat16)
    row_dot = jnp.einsum("tkgd,tkgd->kgt", d_attended.astype(jnp.float32), attended)
    keys_back, values_back = (
        lax.all_gather(keys_own, "ctx", axis=0, tiled=True),
        lax.all_gather(values_own, "ctx", axis=0, tiled=True),
    )
    d_queries, d_keys_all, d_values_all = attend_back(
        queries, keys_back, values_back, first_row, key_block, log_total, d_attended, row_dot
    )
    d_keys, d_values = (
        lax.psum_scatter(
            d_keys_all.astype(jnp.bfloat16), "ctx", scatter_dimension=0, tiled=True
        ).astype(jnp.float32),
        lax.psum_scatter(
            d_values_all.astype(jnp.bfloat16), "ctx", scatter_dimension=0, tiled=True
        ).astype(jnp.float32),
    )
    d_query_rot = rope_back(d_queries.reshape(rows_here, H, HD), cosine, sine)
    grad_gain_q = jnp.sum(d_query_rot * unit_query, axis=(0, 1))
    d_query_raw = (
        norm_back(d_query_rot * attn_back[5].astype(jnp.float32), query_heads)
        .reshape(rows_here, H * HD)
        .astype(jnp.bfloat16)
    )
    d_key_rot = rope_back(d_keys, cosine, sine)
    grad_gain_k = jnp.sum(d_key_rot * unit_key, axis=(0, 1))
    d_key_raw = (
        norm_back(d_key_rot * attn_back[6].astype(jnp.float32), key_heads)
        .reshape(rows_here, KV * HD)
        .astype(jnp.bfloat16)
    )
    d_value_raw = d_values.reshape(rows_here, KV * HD).astype(jnp.bfloat16)
    d_normed_in = contract_cols(d_query_raw, attn_back[1]) + contract_cols(d_key_raw, attn_back[2])
    d_normed_in = (
        d_normed_in
        + contract_cols(d_value_raw, attn_back[3])
        + contract_cols(d_gate_logit, attn_back[4])
    )
    grad_gain_one = jnp.sum(d_normed_in * unit_in, axis=0)
    grad_inputs = d_middle + norm_back(d_normed_in * attn_back[0].astype(jnp.float32), hidden_in)
    grad_query_full = contract_rows(normed_in, d_query_raw)
    grad_key_full = contract_rows(normed_in, d_key_raw)
    grad_value_full = contract_rows(normed_in, d_value_raw)
    grad_logit_full = contract_rows(normed_in, d_gate_logit)
    grad_terms = (
        grad_gain_one,
        grad_query_full,
        grad_key_full,
        grad_value_full,
        grad_logit_full,
        grad_gain_q,
        grad_gain_k,
        grad_out_full,
        grad_gain_two,
        grad_down_full,
    )
    shares = (
        lax.psum_scatter(grad_terms[0], ("dp", "ctx"), scatter_dimension=0, tiled=True),
        lax.psum_scatter(grad_terms[1], ("dp", "ctx"), scatter_dimension=0, tiled=True),
        lax.psum_scatter(grad_terms[2], ("dp", "ctx"), scatter_dimension=0, tiled=True),
        lax.psum_scatter(grad_terms[3], ("dp", "ctx"), scatter_dimension=0, tiled=True),
        lax.psum_scatter(grad_terms[4], ("dp", "ctx"), scatter_dimension=0, tiled=True),
        lax.psum_scatter(grad_terms[5], ("dp", "ctx"), scatter_dimension=0, tiled=True),
        lax.psum_scatter(grad_terms[6], ("dp", "ctx"), scatter_dimension=0, tiled=True),
        lax.psum_scatter(grad_terms[7], ("dp", "ctx"), scatter_dimension=1, tiled=True),
        lax.psum_scatter(grad_terms[8], ("dp", "ctx"), scatter_dimension=0, tiled=True),
        lax.psum_scatter(grad_terms[9], ("dp", "ctx"), scatter_dimension=1, tiled=True),
    )
    ffn_width = w_gate.shape[1]
    return (
        result.astype(jnp.bfloat16)[None],
        loss,
        grad_inputs[None],
        shares[0],
        shares[1],
        shares[2],
        shares[3],
        shares[4],
        shares[5],
        shares[6],
        shares[7],
        shares[8],
        gate_up_share[:, :ffn_width],
        gate_up_share[:, ffn_width:],
        shares[9],
    )


def solution(mesh):
    placed = (
        P("dp", "ctx", None),
        P("dp", "ctx", None),
        P("dp", "ctx"),
        P("dp", "ctx"),
        P(("dp", "ctx")),
        P(("dp", "ctx"), None),
        P(("dp", "ctx"), None),
        P(("dp", "ctx"), None),
        P(("dp", "ctx"), None),
        P(("dp", "ctx")),
        P(("dp", "ctx")),
        P(None, ("dp", "ctx")),
        P(("dp", "ctx")),
        P(("dp", "ctx"), None),
        P(("dp", "ctx"), None),
        P(None, ("dp", "ctx")),
    )
    return jax.shard_map(
        on_device,
        mesh=mesh,
        in_specs=placed,
        out_specs=(
            P("dp", "ctx", None),
            P(),
            P("dp", "ctx", None),
            P(("dp", "ctx")),
            P(("dp", "ctx"), None),
            P(("dp", "ctx"), None),
            P(("dp", "ctx"), None),
            P(("dp", "ctx"), None),
            P(("dp", "ctx")),
            P(("dp", "ctx")),
            P(None, ("dp", "ctx")),
            P(("dp", "ctx")),
            P(("dp", "ctx"), None),
            P(("dp", "ctx"), None),
            P(None, ("dp", "ctx")),
        ),
        check_vma=False,
    )
```

profile of v0, /device:TPU:8, one launch (start us, length us, event | category | flops | bytes accessed | tf_op | source)
XLA Modules:
  0.0 3246.8 jit_solution(15554003775514122847)
XLA Ops:
  12.8 41.0 %all-reduce.9 = (bf16[2048]{0:T(1024)(128)(2,1)S(1)}, bf16[128]{0:T(256)(128)(2,1)S(1)}, bf16[128]{0:T(256)(128)(2,1)S(1)}, bf16[2048]{0:T(1024)(128)(2,1)S(1)}) all-reduce(bf16[2048]{0:T(1024)(128)(2,1)S(1)} %dynamic-update-slice, bf16[128]{0:T(256)(128)(2,1)S(1)} %dynamic-update-slice.1, ...), channel_id=1, replica_groups=mesh['dp'=4,'ctx'=8] {'dp','ctx'}, use_global_device_ids=true, to_apply=%add | all-reduce | flops 4352 | bytes 17408
  55.8 18.6 all-gather.15.cloned.1.call-done
  74.4 6.6 copy.67
  81.0 3.6 multiply_reduce_fusion.11
  87.3 50.8 %all-gather.11.cloned.1.call-done = bf16[2048,1024]{1,0:T(8,128)(2,1)} async-done(((bf16[64,1024]{1,0:T(8,128)(2,1)}), bf16[2048,1024]{1,0:T(8,128)(2,1)}) %all-gather.11.cloned.1.call-update) | async-done | bytes 4194320 | tf_op jit(solution)/shard_map/all_gather | solution.py:182
  138.1 6.5 copy.66
  144.6 4.5 convolution_convert_fusion
  152.6 43.0 %psum.15 = f32[]{:T(128)} all-reduce(f32[]{:T(128)} %convert_reduce_fusion), channel_id=1, replica_groups=mesh['dp'=4,'ctx'=8] {'dp','ctx'}, use_global_device_ids=true, to_apply=%region_14.15 | all-reduce | flops 1 | bytes 8 | tf_op jit(solution)/shard_map/psum | solution.py:241
  195.7 38.4 %all-gather = bf16[32,64,16]{1,2,0:T(8,128)(2,1)S(1)} all-gather(bf16[1,64,16]{1,2,0:T(8,128)(2,1)S(1)} %bitcast.330), channel_id=1, replica_groups=mesh['dp'=4,'ctx'=8] {'dp','ctx'}, dimensions={0}, use_global_device_ids=true | all-gather | bytes 67584 | tf_op jit(solution)/shard_map/all_gather | solution.py:183
  236.2 6.5 copy.72
  242.7 24.2 all-gather.19.cloned.1.call-done
  266.9 12.4 copy.68
  279.2 6.0 multiply_reduce_fusion.8
  287.9 9.8 while.36
  288.0 2.6 fusion.184
  292.9 2.6 fusion.184
  297.7 15.4 all-gather.13.cloned.1.call-done
  314.6 12.2 while.37
  314.7 5.9 bitcast_add_fusion.4
  320.8 5.9 bitcast_add_fusion.4
  329.2 64.5 %all-gather.21.cloned.1.call-done = bf16[2048,2048]{0,1:T(8,128)(2,1)} async-done(((bf16[2048,64]{0,1:T(8,128)(2,1)}), bf16[2048,2048]{0,1:T(8,128)(2,1)}) %all-gather.21.cloned.1.call-update) | async-done | bytes 8388624 | tf_op jit(solution)/shard_map/all_gather | solution.py:186
  393.6 5.9 multiply_reduce_fusion.7
  401.2 146.9 %all-gather.23.cloned.1.call-done = bf16[2048,6144]{1,0:T(8,128)(2,1)} async-done(((bf16[64,6144]{1,0:T(8,128)(2,1)}), bf16[2048,6144]{1,0:T(8,128)(2,1)}) %all-gather.23.cloned.1.call-update) | async-done | bytes 25165840 | tf_op jit(solution)/shard_map/all_gather | solution.py:190
  548.1 14.3 fusion.111
  562.4 141.6 %all-gather.25.cloned.1.call-done = bf16[2048,6144]{1,0:T(8,128)(2,1)} async-done(((bf16[64,6144]{1,0:T(8,128)(2,1)}), bf16[2048,6144]{1,0:T(8,128)(2,1)}) %all-gather.25.cloned.1.call-update) | async-done | bytes 25165840 | tf_op jit(solution)/shard_map/all_gather | solution.py:191
  704.0 19.4 multiply_convert_fusion.2
  723.3 136.5 %all-gather.27.cloned.1.call-done = bf16[6144,2048]{0,1:T(8,128)(2,1)} async-done(((bf16[6144,64]{0,1:T(8,128)(2,1)}), bf16[6144,2048]{0,1:T(8,128)(2,1)}) %all-gather.27.cloned.1.call-update) | async-done | bytes 25165840 | tf_op jit(solution)/shard_map/all_gather | solution.py:192
  859.9 14.2 fusion.76
  874.0 21.7 multiply_convert_fusion
  895.7 13.7 fusion.112
  909.4 15.0 multiply_reduce_fusion.1
  924.5 5.7 multiply_add_fusion.1
  931.5 5.8 fusion.96
  937.3 2.8 reshape.253
  940.1 3.3 bitcast_convert_fusion
  943.4 3.1 copy.97
  953.6 51.0 %while.38 = (s32[]{:T(128)}, f32[256,8,2,128]{0,3,2,1:T(8,128)S(1)}, bf16[2048,8,128]{0,2,1:T(8,128)(2,1)}, bf16[2048,8,128]{0,2,1:T(8,128)(2,1)}, s32[]{:T(128)...) while((s32[]{:T(128)}, ...), condition=%wide.region_17.18_spmd, body=%wide.region_16.17_spmd.sunk | while | flops 2707555072 | bytes 81189128 | solution.py:157
  958.9 5.3 fusion.200
  966.5 4.6 fusion.202
  975.9 3.1 constant_dynamic-update-slice_fusion.3
  984.3 5.3 fusion.200
  991.9 4.6 fusion.202
  1001.2 3.2 constant_dynamic-update-slice_fusion.3
  1014.6 21.2 fusion.115
  1035.8 21.2 fusion.114
  1057.1 65.9 %pad_maximum_fusion = f32[2048,12288]{1,0:T(8,128)} fusion(f32[2048,6144]{1,0:T(8,128)} %fusion.115, f32[2048,6144]{1,0:T(8,128)} %fusion.114), kind=kLoop, calls=%fused_computation.65 | loop fusion | flops 25165824 | bytes 201326592 | tf_op jit(solution)/shard_map/concatenate | solution.py:269
  1123.1 5.7 fusion.90
  1129.3 22.9 reduce-scatter.12.cloned.1.call-done
  1154.4 4.6 fusion.88
  1160.6 9.4 fusion.94
  1175.0 8.2 fusion.92
  1183.5 21.2 fusion.116
  1205.9 7.2 fusion.113
  1213.1 73.3 %reduce-scatter.28.cloned.1.call-done = f32[64,16]{1,0:T(8,128)} async-done(((f32[2048,16]{1,0:T(8,128)}), f32[64,16]{1,0:T(8,128)}) %reduce-scatter.28.cloned.1.call-update) | async-done | bytes 4112
  1287.8 4.3 convolution_add_fusion.4
  1295.5 44.1 %all-reduce.8 = (f32[]{:T(128)}, f32[2048]{0:T(1024)S(1)}, f32[128]{0:T(128)S(1)}, f32[128]{0:T(128)S(1)}, f32[2048]{0:T(1024)S(1)}) all-reduce(f32[]{:T(128)} %multiply_reduce_fusion.12, f32[2048]{0:T(1024)S(1)} %get-tuple-element.253, f32[128]{0:T(128)S(1)} %get-tuple-element.249, ...), channel_id=1, replica_groups=mesh['dp'=4,'ctx'=8] {'dp','ctx'}, use_global_device_ids=true, to_apply=%region_12.13 | all-reduce | flops 4353 | bytes 34824 | tf_op jit(solution)/shard_map/psum | solution.py:241
  1343.3 3.9 fusion.67
  1347.1 773.9 %reduce-scatter.24.cloned.1.call-done = f32[64,12288]{1,0:T(8,128)} async-done(((f32[2048,12288]{1,0:T(8,128)}), f32[64,12288]{1,0:T(8,128)}) %reduce-scatter.24.cloned.1.call-update) | async-done | bytes 3145744 | tf_op jit(solution)/shard_map/reduce_scatter | solution.py:268
  2121.0 3.8 fusion.108
  2124.9 145.5 %reduce-scatter.20.cloned.1.call-done = f32[64,1024]{1,0:T(8,128)} async-done(((f32[2048,1024]{1,0:T(8,128)}), f32[64,1024]{1,0:T(8,128)}) %reduce-scatter.20.cloned.1.call-update) | async-done | bytes 262160 | tf_op jit(solution)/shard_map/reduce_scatter | solution.py:347
  2270.3 152.8 %reduce-scatter.18.cloned.1.call-done = f32[64,1024]{1,0:T(8,128)} async-done(((f32[2048,1024]{1,0:T(8,128)}), f32[64,1024]{1,0:T(8,128)}) %reduce-scatter.18.cloned.1.call-update) | async-done | bytes 262160 | tf_op jit(solution)/shard_map/reduce_scatter | solution.py:346
  2423.1 186.2 %reduce-scatter.22.cloned.1.call-done = f32[2048,64]{0,1:T(8,128)} async-done(((f32[2048,2048]{0,1:T(8,128)}), f32[2048,64]{0,1:T(8,128)}) %reduce-scatter.22.cloned.1.call-update) | async-done | bytes 524304 | tf_op jit(solution)/shard_map/reduce_scatter | solution.py:351
  2609.4 187.2 %reduce-scatter.16.cloned.1.call-done = f32[64,2048]{1,0:T(8,128)} async-done(((f32[2048,2048]{1,0:T(8,128)}), f32[64,2048]{1,0:T(8,128)}) %reduce-scatter.16.cloned.1.call-update) | async-done | bytes 524304 | tf_op jit(solution)/shard_map/reduce_scatter | solution.py:345
  2796.6 442.1 %reduce-scatter.26.cloned.1.call-done = f32[6144,64]{0,1:T(8,128)} async-done(((f32[6144,2048]{0,1:T(8,128)}), f32[6144,64]{0,1:T(8,128)}) %reduce-scatter.26.cloned.1.call-update) | async-done | bytes 1572880 | tf_op jit(solution)/shard_map/reduce_scatter | solution.py:353
  (268 shorter events, 88.5 us)
Async XLA Ops:
  7.2 67.3 %all-gather.15.cloned.1.call-start = ((), (), s32[]{:S(2)}) async-start(), calls=%async_computation.11 | async-start | bytes 4325376 | tf_op jit(solution)/shard_map/all_gather | solution.py:181
  7.9 130.2 %all-gather.11.cloned.1.call-start = ((), (), s32[]{:S(2)}) async-start(), calls=%async_computation.9 | async-start | bytes 4325376 | tf_op jit(solution)/shard_map/all_gather | solution.py:182
  8.7 227.5 %all-gather.17.cloned.1.call-start = ((), (), s32[]{:S(2)}) async-start(), calls=%async_computation.12 | async-start | bytes 4718592 | tf_op jit(solution)/shard_map/all_gather | solution.py:221
  53.8 31.1 copy-start.53
  53.8 225.4 %copy-start.30 = (f32[2048]{0:T(1024)}, f32[2048]{0:T(1024)S(1)}, u32[]{:S(2)}) copy-start(f32[2048]{0:T(1024)S(1)} %convert_element_type.151) | copy-start | bytes 24580
  54.2 231.6 %copy-start.21 = (f32[256,128]{0,1:T(8,128)}, f32[256,128]{0,1:T(8,128)S(1)}, u32[]{:S(2)}) copy-start(f32[256,128]{0,1:T(8,128)S(1)} %get-tuple-element.356) | copy-start | bytes 393220
  54.2 231.6 %copy-start.27 = (f32[256,128]{0,1:T(8,128)}, f32[256,128]{0,1:T(8,128)S(1)}, u32[]{:S(2)}) copy-start(f32[256,128]{0,1:T(8,128)S(1)} %get-tuple-element.357) | copy-start | bytes 393220
  55.8 223.4 %copy-start.43 = (f32[256]{0:T(256)}, f32[256]{0:T(256)S(1)}, u32[]{:S(2)}) copy-start(f32[256]{0:T(256)S(1)} %add_rsqrt_fusion.3) | copy-start | bytes 3076
  74.4 6.6 copy-start.3
  86.7 180.2 %all-gather.19.cloned.1.call-start = ((), (), s32[]{:S(2)}) async-start(), calls=%async_computation.13 | async-start | bytes 8650752 | tf_op jit(solution)/shard_map/all_gather | solution.py:180
  87.3 225.8 %all-gather.13.cloned.1.call-start = ((), (), s32[]{:S(2)}) async-start(), calls=%async_computation.10 | async-start | bytes 4718592 | tf_op jit(solution)/shard_map/all_gather | solution.py:222
  149.1 2.9 copy-start.59
  149.1 46.6 %copy-start.58 = (bf16[64,16]{0,1:T(8,128)(2,1)S(1)}, bf16[64,16]{0,1:T(8,128)(2,1)}, u32[]{:S(2)}) copy-start(bf16[64,16]{0,1:T(8,128)(2,1)} %param.30) | copy-start | bytes 6148
  149.2 244.5 %all-gather.21.cloned.1.call-start = ((), (), s32[]{:S(2)}) async-start(), calls=%async_computation.14 | async-start | bytes 8650752 | tf_op jit(solution)/shard_map/all_gather | solution.py:186
  149.8 398.3 %all-gather.23.cloned.1.call-start = ((), (), s32[]{:S(2)}) async-start(), calls=%async_computation.15 | async-start | bytes 25952256 | tf_op jit(solution)/shard_map/all_gather | solution.py:190
  150.5 553.5 %all-gather.25.cloned.1.call-start = ((), (), s32[]{:S(2)}) async-start(), calls=%async_computation.16 | async-start | bytes 25952256 | tf_op jit(solution)/shard_map/all_gather | solution.py:191
  151.3 708.6 %all-gather.27.cloned.1.call-start = ((), (), s32[]{:S(2)}) async-start(), calls=%async_computation.17 | async-start | bytes 25952256 | tf_op jit(solution)/shard_map/all_gather | solution.py:192
  152.0 971.1 %reduce-scatter.14.cloned.1.call-start = ((), (), s32[]{:S(2)}) async-start(), calls=%async_computation.19 | async-start | bytes 4718592 | tf_op jit(solution)/shard_map/reduce_scatter | solution.py:300
  195.7 728.8 %copy-start.50 = (f32[1,256]{1,0:T(1,128)}, f32[1,256]{1,0:T(1,128)S(1)}, u32[]{:S(2)}) copy-start(f32[1,256]{1,0:T(1,128)S(1)} %convert_element_type.167) | copy-start | bytes 3076
  195.7 90.1 %copy-start.55 = (f32[128]{0:T(128)}, f32[128]{0:T(128)S(1)}, u32[]{:S(2)}) copy-start(f32[128]{0:T(128)S(1)} %convert_element_type.159) | copy-start | bytes 1540
  234.4 8.3 copy-start.37
  234.8 92.6 %copy-start.41 = (f32[256,16]{0,1:T(8,128)}, f32[256,16]{0,1:T(8,128)S(1)}, u32[]{:S(2)}) copy-start(f32[256,16]{0,1:T(8,128)S(1)} %fusion.79) | copy-start | bytes 49156
  329.2 70.4 %copy-start.26 = (bf16[256,2048]{0,1:T(8,128)(2,1)}, bf16[256,2048]{0,1:T(8,128)(2,1)S(1)}, u32[]{:S(2)}) copy-start(bf16[256,2048]{0,1:T(8,128)(2,1)S(1)} %fusion.74) | copy-start | bytes 3145732
  399.6 1.4 copy-start.19
  401.2 302.8 %copy-start.15 = (bf16[256,2048]{1,0:T(8,128)(2,1)}, bf16[256,2048]{1,0:T(8,128)(2,1)S(1)}, u32[]{:S(2)}) copy-start(bf16[256,2048]{1,0:T(8,128)(2,1)S(1)} %multiply_convert_fusion.4) | copy-start | bytes 3145732
  562.4 297.5 %copy-start.33 = (bf16[1,256,2048]{2,1,0:T(8,128)(2,1)S(1)}, bf16[1,256,2048]{2,1,0:T(8,128)(2,1)}, u32[]{:S(2)}) copy-start(bf16[1,256,2048]{2,1,0:T(8,128)(2,1)} %param.23) | copy-start | bytes 3145732
  874.0 21.7 copy-start.34
  895.7 13.7 copy-start.20
  937.3 2.8 copy-start.17
  937.3 2.8 copy-start.47
  943.4 3.1 copy-start.7
  951.1 2.5 copy-start.49
  953.8 2.6 copy-start.32
  966.5 4.6 copy-start
  979.1 2.6 copy-start.32
  991.9 4.6 copy-start
  1005.9 146.3 %reduce-scatter.12.cloned.1.call-start = ((), (), s32[]{:S(2)}) async-start(), calls=%async_computation.18 | async-start | bytes 4718592 | tf_op jit(solution)/shard_map/reduce_scatter | solution.py:297
  1005.9 1.6 copy-start.8
  1006.6 279.7 %reduce-scatter.28.cloned.1.call-start = ((), (), s32[]{:S(2)}) async-start(), calls=%async_computation.26 | async-start | bytes 1081344
  1009.5 2.2 copy-start.18
  1012.3 2.2 copy-start.16
  1012.9 22.9 copy-start.45
  1057.1 1063.9 %reduce-scatter.24.cloned.1.call-start = ((), (), s32[]{:S(2)}) async-start(), calls=%async_computation.24 | async-start | bytes 103809024 | tf_op jit(solution)/shard_map/reduce_scatter | solution.py:268
  1123.0 1147.3 %reduce-scatter.20.cloned.1.call-start = ((), (), s32[]{:S(2)}) async-start(), calls=%async_computation.22 | async-start | bytes 8650752 | tf_op jit(solution)/shard_map/reduce_scatter | solution.py:347
  1128.8 23.4 copy-start.28
  1128.8 24.7 copy-start.13
  1128.8 24.7 copy-start.22
  1128.8 24.7 copy-start.40
  1128.9 24.7 copy-start.54
  1128.9 1294.3 %reduce-scatter.18.cloned.1.call-start = ((), (), s32[]{:S(2)}) async-start(), calls=%async_computation.21 | async-start | bytes 8650752 | tf_op jit(solution)/shard_map/reduce_scatter | solution.py:346
  1154.3 4.7 copy-start.23
  1159.0 1.6 copy-start.10
  1159.0 1450.4 %reduce-scatter.22.cloned.1.call-start = ((), (), s32[]{:S(2)}) async-start(), calls=%async_computation.23 | async-start | bytes 17301504 | tf_op jit(solution)/shard_map/reduce_scatter | solution.py:351
  1169.9 1.6 copy-start.2
  1170.0 1626.6 %reduce-scatter.16.cloned.1.call-start = ((), (), s32[]{:S(2)}) async-start(), calls=%async_computation.20 | async-start | bytes 17301504 | tf_op jit(solution)/shard_map/reduce_scatter | solution.py:345
  1171.8 1.6 copy-start.6
  1171.8 1.6 copy-start.36
  1171.8 1.6 copy-start.56
  1183.2 2055.4 %reduce-scatter.26.cloned.1.call-start = ((), (), s32[]{:S(2)}) async-start(), calls=%async_computation.25 | async-start | bytes 51904512 | tf_op jit(solution)/shard_map/reduce_scatter | solution.py:353
  1205.9 81.9 %copy-start.24 = (bf16[256,8,128]{0,2,1:T(8,128)(2,1)S(1)}, bf16[256,8,128]{0,2,1:T(8,128)(2,1)}, u32[]{:S(2)}) copy-start(bf16[256,8,128]{0,2,1:T(8,128)(2,1)} %copy-done.23) | copy-start | bytes 1572868
  1287.8 4.3 copy-start.14
  1287.8 4.3 copy-start.29
  1293.5 2.1 copy-start.52
  1293.5 49.8 %copy-start.11 = (f32[256,2048]{1,0:T(8,128)S(1)}, f32[256,2048]{1,0:T(8,128)}, u32[]{:S(2)}) copy-start(f32[256,2048]{1,0:T(8,128)} %copy-done.9) | copy-start | bytes 6291460
  (16 other events, 17.6 us)
Sparse Core Ops, SparseCore 0:
  11.0 63.3 all-gather.14
  77.4 60.6 all-gather.10
  140.3 46.5 all-gather.16
  189.8 77.0 all-gather.18
  268.9 44.1 all-gather.12
  315.9 77.7 all-gather.20
  396.7 151.3 all-gather.22
  551.1 152.8 all-gather.24
  707.0 152.8 all-gather.26
  1004.7 96.9 reduce-scatter.13
  1104.0 48.1 reduce-scatter.11
  1154.9 131.4 reduce-scatter.27
  1293.9 827.0 reduce-scatter.23
  2123.8 146.4 reduce-scatter.19
  2273.1 149.9 reduce-scatter.17
  2426.0 183.3 reduce-scatter.21
  2612.2 184.3 reduce-scatter.15
  2804.6 434.0 reduce-scatter.25
where the time goes:
time: 3260 us; the launch traced here: 3250 us
  waiting for transfers between devices  2590 us (79%)
  matrix products  284 us (9%)
  blocking collectives  167 us (5%)
  other arithmetic  98.8 us (3%)
  local copies, waits for them, and re-layouts  89.2 us (3%)
    reduce_scatter x1, waiting for transfers between devices, on_device(): lax.psum_scatter(jnp.concatenate([contract_rows(normed_mid, d_gate), cont...  774 us
    reduce_scatter x1, waiting for transfers between devices, on_device(): lax.psum_scatter(grad_terms[9], ('dp', 'ctx'), scatter_dimension=1, tiled...  442 us
    reduce_scatter x1, waiting for transfers between devices, on_device(): lax.psum_scatter(grad_terms[1], ('dp', 'ctx'), scatter_dimension=0, tiled...  187 us
    reduce_scatter x1, waiting for transfers between devices, on_device(): lax.psum_scatter(grad_terms[7], ('dp', 'ctx'), scatter_dimension=1, tiled...  186 us
    reduce_scatter x1, waiting for transfers between devices, on_device(): lax.psum_scatter(grad_terms[2], ('dp', 'ctx'), scatter_dimension=0, tiled...  153 us
    all_gather x1, waiting for transfers between devices, on_device(): lax.all_gather(w_gate, ('dp', 'ctx'), axis=0, tiled=True)  147 us
    reduce_scatter x1, waiting for transfers between devices, on_device(): lax.psum_scatter(grad_terms[3], ('dp', 'ctx'), scatter_dimension=0, tiled...  145 us
    all_gather x1, waiting for transfers between devices, on_device(): lax.all_gather(w_up, ('dp', 'ctx'), axis=0, tiled=True)  142 us
  transfers between devices with their start and end apart: 18, of which 16 were waited for; matrix products, arithmetic and copies ran while one was open for 10% of the time, Pallas kernels for 0%

commit v1 on v0

--- a/solution.py
+++ b/solution.py
@@ -1,8 +1,10 @@
+import functools
 import math
 
 import jax
 import jax.numpy as jnp
 from jax import lax
+from jax.sharding import Mesh
 from jax.sharding import PartitionSpec as P
 
 H = 16
@@ -13,6 +15,8 @@
 EPSILON = 1e-06
 ROPE_BASE = 1000000.0
 MASKED = -1e30
+PLANE = ("dp", "core")
+EVERY = ("dp", "z", "core")
 
 
 def normalize(values):
@@ -62,6 +66,22 @@
     return lax.dot_general(
         left, right, (((1,), (1,)), ((), ())), preferred_element_type=jnp.float32
     )
+
+
+def matmul(left, right):
+    return jnp.dot(left, right, preferred_element_type=jnp.float32)
+
+
+def plane_gather(rows):
+    return lax.all_gather(rows, PLANE, axis=0, tiled=True)
+
+
+def plane_sum(partial):
+    return lax.psum_scatter(partial, PLANE, scatter_dimension=0, tiled=True)
+
+
+def column_swap(values):
+    return lax.all_to_all(values, "z", 0, 0, tiled=True)
 
 
 def block_scores(queries, keys_all, values_all, first_row, step_index, key_block):
@@ -157,7 +177,7 @@
     return lax.fori_loop(0, blocks_needed, accumulate, start_state)
 
 
-def on_device(
+def weight_gathered(
     inputs,
     targets,
     valid,
@@ -372,45 +392,321 @@
     )
 
 
+def tensor_parallel(
+    dp_n,
+    z_n,
+    inputs,
+    targets,
+    valid,
+    positions,
+    ln1_gain,
+    w_query,
+    w_key,
+    w_value,
+    w_gatelogit,
+    q_gain,
+    k_gain,
+    w_output,
+    ln2_gain,
+    w_gate,
+    w_up,
+    w_down,
+):
+    plane_n = dp_n * 2
+    rows_here, width = inputs.shape[1:]
+    piece = ln1_gain.shape[0]
+    group = KV // plane_n
+    q_heads = H // plane_n
+    q_cols, k_cols = q_heads * HD, group * HD
+    ff_cols = w_gate.shape[1] // plane_n
+    tokens = plane_n * rows_here
+    plane_at = lax.axis_index("dp") * 2 + lax.axis_index("core")
+
+    def to_inner(values):
+        lead = values.shape[:-1]
+        blocks = values.reshape(lead + (dp_n, z_n, 2 * piece))
+        return jnp.swapaxes(blocks, -3, -2).reshape(lead + (width,))
+
+    def to_outer(values):
+        lead = values.shape[:-1]
+        blocks = values.reshape(lead + (z_n, dp_n, 2 * piece))
+        return jnp.swapaxes(blocks, -3, -2).reshape(lead + (width,))
+
+    whole_parts = jnp.concatenate([positions[0], jnp.sum(valid[0])[None].astype(jnp.int32)])
+    whole_all = lax.all_gather(whole_parts, EVERY, axis=0).reshape(dp_n, z_n, 2, rows_here + 1)
+    valid_count = jnp.sum(whole_all[..., -1]).astype(jnp.float32)
+    places = lax.dynamic_index_in_dim(whole_all, lax.axis_index("z"), 1, False)
+    places = places[..., :rows_here].reshape(tokens)
+
+    small = jnp.concatenate([ln1_gain, ln2_gain, w_gatelogit.reshape(-1), q_gain, k_gain])
+    small_all = lax.all_gather(small, EVERY, axis=0)
+    small_inner = jnp.swapaxes(small_all.reshape(dp_n, z_n, 2, -1), 0, 1).reshape(
+        small_all.shape
+    )
+    gain_one = small_inner[:, :piece].reshape(width).astype(jnp.float32)
+    gain_two = small_inner[:, piece : 2 * piece].reshape(width).astype(jnp.float32)
+    logit_end = 2 * piece + piece * H
+    w_logit = small_inner[:, 2 * piece : logit_end].reshape(width, H)
+    w_logit = lax.dynamic_slice_in_dim(w_logit, plane_at * q_heads, q_heads, 1)
+    head_piece = q_gain.shape[0]
+    gain_q = small_all[:, logit_end : logit_end + head_piece].reshape(HD).astype(jnp.float32)
+    gain_k = small_all[:, logit_end + head_piece :].reshape(HD).astype(jnp.float32)
+
+    def by_plane(weight):
+        return jnp.swapaxes(weight.reshape(piece, plane_n, -1), 0, 1)
+
+    attn_parts = jnp.concatenate(
+        [by_plane(w_query), by_plane(w_key), by_plane(w_value), by_plane(w_output.T)], axis=2
+    )
+    ffn_parts = jnp.concatenate([by_plane(w_gate), by_plane(w_up), by_plane(w_down.T)], axis=2)
+
+    def assemble(parts):
+        mine = lax.all_to_all(parts, PLANE, 0, 0, tiled=True)
+        mine = mine.reshape(plane_n * piece, parts.shape[2])
+        return lax.all_gather(mine, "z", axis=0, tiled=True)
+
+    attn_w = assemble(attn_parts)
+    ffn_w = assemble(ffn_parts)
+    w_qkv = attn_w[:, : q_cols + 2 * k_cols]
+    w_out_t = attn_w[:, q_cols + 2 * k_cols :]
+    w_gate_up = ffn_w[:, : 2 * ff_cols]
+    w_down_t = ffn_w[:, 2 * ff_cols :]
+
+    hidden_in = to_inner(inputs[0]).astype(jnp.float32)
+    unit_in = normalize(hidden_in)
+    normed_in = (unit_in * gain_one).astype(jnp.bfloat16)
+    normed_all = plane_gather(normed_in)
+    cosine, sine = rope_tables(places)
+    qkv_raw = matmul(normed_all, w_qkv)
+    gate_logit = matmul(normed_all, w_logit)
+    query_heads = qkv_raw[:, :q_cols].reshape(tokens, q_heads, HD)
+    key_heads = qkv_raw[:, q_cols : q_cols + k_cols].reshape(tokens, group, HD)
+    unit_query = normalize(query_heads)
+    unit_key = normalize(key_heads)
+    queries = apply_rope(unit_query * gain_q, cosine, sine).astype(jnp.bfloat16)
+    keys = apply_rope(unit_key * gain_k, cosine, sine).astype(jnp.bfloat16)
+    sent = jnp.concatenate(
+        [
+            queries.reshape(tokens, q_cols),
+            keys.reshape(tokens, k_cols),
+            qkv_raw[:, q_cols + k_cols :].astype(jnp.bfloat16),
+        ],
+        axis=1,
+    )
+    held = column_swap(sent)
+    queries = held[:, :q_cols].reshape(tokens, group, q_heads // group, HD)
+    keys = held[:, q_cols : q_cols + k_cols].reshape(tokens, group, HD)
+    values = held[:, q_cols + k_cols :].reshape(tokens, group, HD)
+    causal = lax.iota(jnp.int32, tokens)[None, :] <= lax.iota(jnp.int32, tokens)[:, None]
+    score_scale = HD ** (-0.5)
+    scores = (
+        jnp.einsum("tkgd,skd->kgts", queries, keys, preferred_element_type=jnp.float32)
+        * score_scale
+    )
+    scores = jnp.where(causal, scores, MASKED)
+    log_total = jax.nn.logsumexp(scores, axis=-1)
+    probs = jnp.exp(scores - log_total[..., None])
+    attended = jnp.einsum(
+        "kgts,skd->tkgd", probs.astype(jnp.bfloat16), values, preferred_element_type=jnp.float32
+    )
+    attended_back = column_swap(attended.astype(jnp.bfloat16).reshape(tokens, q_cols))
+    attended_heads = attended_back.reshape(tokens, q_heads, HD).astype(jnp.float32)
+    gate_open = jax.nn.sigmoid(gate_logit)
+    gated = (attended_heads * gate_open[:, :, None]).reshape(tokens, q_cols).astype(jnp.bfloat16)
+    branch = plane_sum(contract_cols(gated, w_out_t).astype(jnp.bfloat16))
+    middle = hidden_in + branch.astype(jnp.float32)
+    unit_mid = normalize(middle)
+    normed_mid = plane_gather((unit_mid * gain_two).astype(jnp.bfloat16))
+    gate_up = matmul(normed_mid, w_gate_up)
+    gate_pre, up_proj = gate_up[:, :ff_cols], gate_up[:, ff_cols:]
+    sigmoid_gate = jax.nn.sigmoid(gate_pre)
+    activated = (gate_pre * sigmoid_gate * up_proj).astype(jnp.bfloat16)
+    branch = plane_sum(contract_cols(activated, w_down_t).astype(jnp.bfloat16))
+    result = middle + branch.astype(jnp.float32)
+
+    weight_rows = valid[0].astype(jnp.float32)
+    difference = result - to_inner(targets[0]).astype(jnp.float32)
+    error_local = jnp.sum(weight_rows * jnp.mean(difference * difference, axis=-1))
+    tokens_all = dp_n * z_n * 2 * rows_here
+    d_result = weight_rows[:, None] * difference * (tokens_all / valid_count)
+    d_branch = plane_gather(d_result.astype(jnp.bfloat16))
+    d_activated = matmul(d_branch, w_down_t)
+    grad_down_t = contract_rows(d_branch, activated).astype(jnp.bfloat16)
+    d_gate = d_activated * up_proj * sigmoid_gate * (1.0 + gate_pre * (1.0 - sigmoid_gate))
+    d_up = d_activated * gate_pre * sigmoid_gate
+    d_gate_up = jnp.concatenate([d_gate, d_up], axis=1).astype(jnp.bfloat16)
+    grad_gate_up = contract_rows(normed_mid, d_gate_up).astype(jnp.bfloat16)
+    d_normed_mid = plane_sum(contract_cols(d_gate_up, w_gate_up).astype(jnp.bfloat16)).astype(
+        jnp.float32
+    )
+    grad_gain_two = jnp.sum(d_normed_mid * unit_mid, axis=0)
+    d_middle = d_result + norm_back(d_normed_mid * gain_two, middle)
+
+    def settle(grads):
+        summed = lax.psum_scatter(grads, "z", scatter_dimension=0, tiled=True)
+        return lax.all_to_all(
+            summed.reshape(plane_n, piece, grads.shape[1]), PLANE, 0, 0, tiled=True
+        )
+
+    def take(settled, start, size):
+        part = jnp.swapaxes(settled[:, :, start : start + size], 0, 1)
+        return part.reshape(piece, plane_n * size).astype(jnp.float32)
+
+    gate_up_own = settle(grad_gate_up)
+    down_own = settle(grad_down_t)
+
+    d_attn = plane_gather(d_middle.astype(jnp.bfloat16))
+    d_gated = matmul(d_attn, w_out_t).reshape(tokens, q_heads, HD)
+    grad_out_t = contract_rows(d_attn, gated).astype(jnp.bfloat16)
+    d_attended = (d_gated * gate_open[:, :, None]).astype(jnp.bfloat16)
+    d_gate_logit = (
+        jnp.sum(d_gated * attended_heads, axis=-1) * gate_open * (1.0 - gate_open)
+    ).astype(jnp.bfloat16)
+    d_attended = column_swap(d_attended.reshape(tokens, q_cols)).reshape(queries.shape)
+    row_dot = jnp.einsum("tkgd,tkgd->kgt", d_attended.astype(jnp.float32), attended)
+    d_probs = jnp.einsum(
+        "tkgd,skd->kgts", d_attended, values, preferred_element_type=jnp.float32
+    )
+    d_scores = (probs * (d_probs - row_dot[..., None])).astype(jnp.bfloat16)
+    d_queries = (
+        jnp.einsum("kgts,skd->tkgd", d_scores, keys, preferred_element_type=jnp.float32)
+        * score_scale
+    )
+    d_keys = (
+        jnp.einsum("kgts,tkgd->skd", d_scores, queries, preferred_element_type=jnp.float32)
+        * score_scale
+    )
+    d_values = jnp.einsum(
+        "kgts,tkgd->skd",
+        probs.astype(jnp.bfloat16),
+        d_attended,
+        preferred_element_type=jnp.float32,
+    )
+    sent = jnp.concatenate(
+        [
+            d_queries.reshape(tokens, q_cols),
+            d_keys.reshape(tokens, k_cols),
+            d_values.reshape(tokens, k_cols),
+        ],
+        axis=1,
+    ).astype(jnp.bfloat16)
+    held = column_swap(sent)
+    d_query_rot = rope_back(
+        held[:, :q_cols].reshape(tokens, q_heads, HD).astype(jnp.float32), cosine, sine
+    )
+    d_key_rot = rope_back(
+        held[:, q_cols : q_cols + k_cols].reshape(tokens, group, HD).astype(jnp.float32),
+        cosine,
+        sine,
+    )
+    grad_gain_q = jnp.sum(d_query_rot * unit_query, axis=(0, 1))
+    grad_gain_k = jnp.sum(d_key_rot * unit_key, axis=(0, 1))
+    d_qkv = jnp.concatenate(
+        [
+            norm_back(d_query_rot * gain_q, query_heads)
+            .reshape(tokens, q_cols)
+            .astype(jnp.bfloat16),
+            norm_back(d_key_rot * gain_k, key_heads).reshape(tokens, k_cols).astype(jnp.bfloat16),
+            held[:, q_cols + k_cols :],
+        ],
+        axis=1,
+    )
+    grad_qkv = contract_rows(normed_all, d_qkv).astype(jnp.bfloat16)
+    grad_logit = contract_rows(normed_all, d_gate_logit)
+    attn_own = settle(jnp.concatenate([grad_qkv, grad_out_t], axis=1))
+    d_normed_in = contract_cols(d_qkv, w_qkv) + contract_cols(d_gate_logit, w_logit)
+    d_normed_in = plane_sum(d_normed_in.astype(jnp.bfloat16)).astype(jnp.float32)
+    grad_gain_one = jnp.sum(d_normed_in * unit_in, axis=0)
+    grad_inputs = d_middle + norm_back(d_normed_in * gain_one, hidden_in)
+
+    devices = dp_n * z_n * 2
+    logit_wide = lax.dynamic_update_slice(
+        jnp.zeros((width, H), jnp.float32), grad_logit, (0, plane_at * q_heads)
+    )
+
+    def outer_rows(values):
+        return jnp.swapaxes(values.reshape(z_n, dp_n, 2, -1), 0, 1).reshape(devices, -1)
+
+    small_sums = jnp.concatenate(
+        [
+            outer_rows(grad_gain_one),
+            outer_rows(grad_gain_two),
+            outer_rows(logit_wide),
+            grad_gain_q.reshape(devices, -1),
+            grad_gain_k.reshape(devices, -1),
+            jnp.full((devices, 1), error_local),
+        ],
+        axis=1,
+    )
+    small_own = lax.psum_scatter(small_sums.reshape(-1), EVERY, scatter_dimension=0, tiled=True)
+    loss = small_own[-1] / valid_count
+    return (
+        to_outer(result.astype(jnp.bfloat16))[None],
+        loss,
+        to_outer(grad_inputs)[None],
+        small_own[:piece],
+        take(attn_own, 0, q_cols),
+        take(attn_own, q_cols, k_cols),
+        take(attn_own, q_cols + k_cols, k_cols),
+        small_own[2 * piece : logit_end].reshape(piece, H),
+        small_own[logit_end : logit_end + head_piece],
+        small_own[logit_end + head_piece : -1],
+        take(attn_own, q_cols + 2 * k_cols, q_cols).T,
+        small_own[piece : 2 * piece],
+        take(gate_up_own, 0, ff_cols),
+        take(gate_up_own, ff_cols, ff_cols),
+        take(down_own, 0, ff_cols).T,
+    )
+
+
 def solution(mesh):
-    placed = (
-        P("dp", "ctx", None),
-        P("dp", "ctx", None),
-        P("dp", "ctx"),
-        P("dp", "ctx"),
-        P(("dp", "ctx")),
-        P(("dp", "ctx"), None),
-        P(("dp", "ctx"), None),
-        P(("dp", "ctx"), None),
-        P(("dp", "ctx"), None),
-        P(("dp", "ctx")),
-        P(("dp", "ctx")),
-        P(None, ("dp", "ctx")),
-        P(("dp", "ctx")),
-        P(("dp", "ctx"), None),
-        P(("dp", "ctx"), None),
-        P(None, ("dp", "ctx")),
-    )
+    dp_n, ctx_n = mesh.shape["dp"], mesh.shape["ctx"]
+    split = ctx_n == 2 * dp_n and KV % (2 * dp_n) == 0
+    if split:
+        mesh = Mesh(mesh.devices.reshape(dp_n, ctx_n // 2, 2), EVERY)
+        on_device = functools.partial(tensor_parallel, dp_n, ctx_n // 2)
+        ctx, every = ("z", "core"), EVERY
+    else:
+        on_device = weight_gathered
+        ctx, every = "ctx", ("dp", "ctx")
+    tokens, rows, cols, flat = P("dp", ctx, None), P(every, None), P(None, every), P(every)
     return jax.shard_map(
         on_device,
         mesh=mesh,
-        in_specs=placed,
+        in_specs=(
+            tokens,
+            tokens,
+            P("dp", ctx),
+            P("dp", ctx),
+            flat,
+            rows,
+            rows,
+            rows,
+            rows,
+            flat,
+            flat,
+            cols,
+            flat,
+            rows,
+            rows,
+            cols,
+        ),
         out_specs=(
-            P("dp", "ctx", None),
+            tokens,
             P(),
-            P("dp", "ctx", None),
-            P(("dp", "ctx")),
-            P(("dp", "ctx"), None),
-            P(("dp", "ctx"), None),
-            P(("dp", "ctx"), None),
-            P(("dp", "ctx"), None),
-            P(("dp", "ctx")),
-            P(("dp", "ctx")),
-            P(None, ("dp", "ctx")),
-            P(("dp", "ctx")),
-            P(("dp", "ctx"), None),
-            P(("dp", "ctx"), None),
-            P(None, ("dp", "ctx")),
+            tokens,
+            flat,
+            rows,
+            rows,
+            rows,
+            rows,
+            flat,
+            flat,
+            cols,
+            flat,
+            rows,
+            rows,
+            cols,
         ),
         check_vma=False,
     )

time: 3260 us -> 1590 us (0.49)
  waiting for transfers between devices: 2590 us -> 1000 us
  blocking collectives: 167 us -> 95.4 us
  starting transfers between devices: 1.26 us -> 38.1 us
    reduce_scatter x8 -> x7, waiting for transfers between devices: 1910 us -> 209 us  [the longest x4 209 us: plane_sum(): return lax.psum_scatter(partial, PLANE, scatter_dimension=0, tiled=True)]
    all_gather x9 -> x6, waiting for transfers between devices: 598 us -> 327 us  [the longest x4 166 us: plane_gather(): return lax.all_gather(rows, PLANE, axis=0, tiled=True)]
    all_to_all x0 -> x7, waiting for transfers between devices: none -> 197 us  [the longest x4 175 us: column_swap(): return lax.all_to_all(values, 'z', 0, 0, tiled=True)]
    unnamed x19 -> x17, waiting for transfers between devices: 78.7 us -> 268 us
    psum x2 -> x0, blocking collectives: 87.1 us -> none  [on_device(): lax.psum((error_local, jnp.sum(weight_rows)), ('dp', 'ctx'))]
    concatenate x1 -> x8, other arithmetic: 65.9 us -> 6.15 us  [the longest x1 1.98 us: tensor_parallel(): attn_own = settle(jnp.concatenate([grad_qkv, grad_out_t], axis=1))]
    all_to_all x0 -> x2, blocking collectives: none -> 56.1 us  [the longest x1 39.6 us: assemble(): mine = lax.all_to_all(parts, PLANE, 0, 0, tiled=True)]
    dot_general x7 -> x5, matrix products: 91.6 us -> 47.9 us  [contract_rows(): lax.dot_general(left, right, (((0,), (0,)), ((), ())), preferred_element_...]
  transfers between devices with their start and end apart: 18 -> 22, of which waited for: 16 -> 17; matrix products, arithmetic and copies ran while one was open for 10% -> 15% of each run, Pallas kernels for 0% -> 0%
where the time goes in v1:
time: 1590 us
  waiting for transfers between devices  1000 us (63%)
  matrix products  257 us (16%)
  local copies, waits for them, and re-layouts  111 us (7%)
  blocking collectives  95.4 us (6%)
  other arithmetic  66.3 us (4%)
  starting transfers between devices  38.1 us (2%)
  between operations  20.1 us (1%)
    unnamed x17, waiting for transfers between devices  268 us
    reduce_scatter x4, waiting for transfers between devices, plane_sum(): return lax.psum_scatter(partial, PLANE, scatter_dimension=0, tiled=True)  209 us
    all_to_all x4, waiting for transfers between devices, column_swap(): return lax.all_to_all(values, 'z', 0, 0, tiled=True)  175 us
    all_gather x4, waiting for transfers between devices, plane_gather(): return lax.all_gather(rows, PLANE, axis=0, tiled=True)  166 us
    all_gather x2, waiting for transfers between devices, assemble(): return lax.all_gather(mine, 'z', axis=0, tiled=True)  161 us
    dot_general x5, matrix products, contract_cols(): lax.dot_general(left, right, (((1,), (1,)), ((), ())), preferred_element_...  60.7 us
    dot_general x5, matrix products, matmul(): return jnp.dot(left, right, preferred_element_type=jnp.float32)  55.1 us
    dot_general x5, matrix products, contract_rows(): lax.dot_general(left, right, (((0,), (0,)), ((), ())), preferred_element_...  47.9 us
  transfers between devices with their start and end apart: 22, of which 17 were waited for; matrix products, arithmetic and copies ran while one was open for 15% of the time, Pallas kernels for 0%

profile of v1, /device:TPU:8, one launch (start us, length us, event | category | flops | bytes accessed | tf_op | source)
XLA Modules:
  0.0 1587.8 jit_solution(4320496693387864526)
XLA Ops:
  13.2 3.7 all-to-all-start
  18.3 11.2 all-to-all-done
  36.5 154.0 %all-reduce.6.cloned.1.call-done = bf16[37120]{0:T(1024)(128)(2,1)} async-done(((bf16[37120]{0:T(1024)(128)(2,1)}), bf16[37120]{0:T(1024)(128)(2,1)}) %all-reduce.6.cloned.1.call-update) | async-done | bytes 74256
  194.6 39.3 %all-reduce.1 = s32[8224]{0:T(1024)S(1)} all-reduce(s32[8224]{0:T(1024)S(1)} %add_dynamic-update-slice_fusion), channel_id=3, replica_groups=mesh['dp'=4,'z'=4,'core'=2] {'dp','z','core'}, use_global_device_ids=true, to_apply=%add.1 | all-reduce | flops 8224 | bytes 65792
  236.6 10.8 all-gather.9.cloned.1.call-done
  247.4 7.6 fusion.45
  260.3 5.7 all-to-all-start.1
  266.0 4.2 iota_compare_fusion
  270.2 41.3 %all-to-all-done.1 = bf16[4,512,512]{1,2,0:T(8,128)(2,1)} async-done(((bf16[4,512,512]{1,2,0:T(8,128)(2,1)}), bf16[4,512,512]{1,2,0:T(8,128)(2,1)}, u32[]{:S(2)}, u32[]{:S(2)}) %all-to-all-start.1) | async-done | bytes 2097184 | tf_op jit(solution)/shard_map/all_to_all | solution.py:84
  311.5 4.1 copy.253
  319.4 16.4 %fusion.3 = (f32[2,2048]{1,0:T(2,128)S(1)}, f32[2048,2048,2]{1,0,2:T(8,128)}) fusion(pred[2048,2048]{0,1:T(8,128)(4,1)} %iota_compare_fusion, bf16[2048,2,128]{0,2,1:T(8,128)(2,1)S(1)} %bitcast.324, bf16[2048,512]{1,0:T(8,128)(2,1)} %bitcast.320), kind=kOutput, calls=%fused_computation.7 | convolution fusion | flops 2172645376 | bytes 39337984 | tf_op jit(solution)/shard_map/tkgd,skd->kgts/dot_general | solution.py:503
  335.8 14.7 exponential_reduce_fusion
  350.5 18.1 %bitcast_convert_fusion = (bf16[2048,1,2,128]{0,3,2,1:T(8,128)(2,1)}, f32[128,2,2048]{2,0,1:T(8,128)}) fusion(f32[2048,2048,2]{1,0,2:T(8,128)} %get-tuple-element.153, f32[2,2048]{1,0:T(2,128)S(1)} %log_add_fusion, pred[2048,2048]{0,1:T(8,128)(4,1)} %iota_compare_fusion, bf16[2048,512]{1,0:T(8,128)(2,1)} %bitcast.321), kind=kOutput, calls=%fused_computation.83 | convolution fusion | flops 2181562368 | bytes 41435136 | tf_op jit(solution)/shard_map/kgts,skd->tkgd/dot_general | solution.py:509
  371.7 7.6 all-to-all-start.2
  379.9 5.9 fusion.25
  387.8 13.7 all-to-all-done.2
  404.1 4.6 mul.466
  411.4 6.9 convolution_convert_fusion.2
  421.5 39.6 %all_to_all.61 = bf16[8,64,2304]{2,1,0:T(8,128)(2,1)} all-to-all(bf16[8,64,2304]{2,1,0:T(8,128)(2,1)S(1)} %copy.261), channel_id=1, replica_groups=mesh['dp'=4,'z'=4,'core'=2] {'dp','core'}, dimensions={0} | all-to-all | bytes 4718592 | tf_op jit(solution)/shard_map/all_to_all | solution.py:464
  461.3 36.8 %reduce-scatter.8.cloned.1.call-done = bf16[256,2048]{1,0:T(8,128)(2,1)} async-done(((bf16[2048,2048]{1,0:T(8,128)(2,1)}), bf16[256,2048]{1,0:T(8,128)(2,1)}) %reduce-scatter.8.cloned.1.call-update) | async-done | bytes 1048592 | tf_op jit(solution)/shard_map/reduce_scatter | solution.py:80
  502.5 160.9 %all-gather.15.cloned.1.call-done = bf16[2048,2304]{1,0:T(8,128)(2,1)} async-done(((bf16[512,2304]{1,0:T(8,128)(2,1)}), bf16[2048,2304]{1,0:T(8,128)(2,1)}) %all-gather.15.cloned.1.call-update) | async-done | bytes 9437200 | tf_op jit(solution)/shard_map/all_gather | solution.py:466
  663.4 58.1 %all-gather.13.cloned.1.call-done = bf16[2048,2048]{1,0:T(8,128)(2,1)} async-done(((bf16[256,2048]{1,0:T(8,128)(2,1)}), bf16[2048,2048]{1,0:T(8,128)(2,1)}) %all-gather.13.cloned.1.call-update) | async-done | bytes 8388624 | tf_op jit(solution)/shard_map/all_gather | solution.py:76
  721.4 17.7 %fusion.7 = f32[2048,1536]{0,1:T(8,128)S(1)} fusion(bf16[2048,2048]{1,0:T(8,128)(2,1)} %all-gather.13.cloned.1.call-done, bf16[2048,2304]{1,0:T(8,128)(2,1)} %all-gather.15.cloned.1.call-done), kind=kOutput, calls=%fused_computation.22 | convolution fusion | flops 12884901888 | bytes 27262976 | tf_op jit(solution)/shard_map/dot_general | solution.py:72
  745.3 11.0 convolution_convert_fusion.1
  761.3 3.7 reshape.483
  765.0 62.5 %reduce-scatter.10.cloned.1.call-done = bf16[256,2048]{1,0:T(8,128)(2,1)} async-done(((bf16[2048,2048]{1,0:T(8,128)(2,1)}), bf16[256,2048]{1,0:T(8,128)(2,1)}) %reduce-scatter.10.cloned.1.call-update) | async-done | bytes 1048592 | tf_op jit(solution)/shard_map/reduce_scatter | solution.py:80
  827.6 3.5 fusion.42
  831.6 53.9 %all-gather.17.cloned.1.call-done = bf16[2048,2048]{1,0:T(8,128)(2,1)} async-done(((bf16[256,2048]{1,0:T(8,128)(2,1)}), bf16[2048,2048]{1,0:T(8,128)(2,1)}) %all-gather.17.cloned.1.call-update) | async-done | bytes 8388624 | tf_op jit(solution)/shard_map/all_gather | solution.py:76
  885.4 16.2 %multiply_convert_fusion.1 = (bf16[2048,768]{0,1:T(8,128)(2,1)S(1)}, bf16[2048,768]{0,1:T(8,128)(2,1)}) fusion(f32[2048,1536]{0,1:T(8,128)} %copy-done.12, bf16[2048,2048]{1,0:T(8,128)(2,1)} %all-gather.17.cloned.1.call-done, bf16[2048,2304]{1,0:T(8,128)(2,1)} %all-gather.15.cloned.1.call-done), kind=kOutput, calls=%fused_computation.18 | convolution fusion | flops 6462898176 | bytes 30408704 | tf_op jit(solution)/shard_map/dot_general | solution.py:72
  903.4 18.5 %convolution_convert_fusion = bf16[2048,2048]{1,0:T(8,128)(2,1)} fusion(bf16[2048,2304]{1,0:T(8,128)(2,1)} %all-gather.15.cloned.1.call-done, bf16[2048,768]{0,1:T(8,128)(2,1)} %get-tuple-element.117, bf16[2048,768]{0,1:T(8,128)(2,1)S(1)} %get-tuple-element.116), kind=kOutput, calls=%fused_computation.12 | convolution fusion | flops 12901679104 | bytes 20971520 | tf_op jit(solution)/shard_map/dot_general | solution.py:66
  922.1 71.1 %reduce-scatter.12.cloned.1.call-done = bf16[256,2048]{1,0:T(8,128)(2,1)} async-done(((bf16[2048,2048]{1,0:T(8,128)(2,1)}), bf16[256,2048]{1,0:T(8,128)(2,1)}) %reduce-scatter.12.cloned.1.call-update) | async-done | bytes 1048592 | tf_op jit(solution)/shard_map/reduce_scatter | solution.py:80
  993.2 3.8 fusion.32
  997.0 3.1 fusion.71
  1000.1 11.4 convolution_convert_fusion.4
  1011.6 42.9 %all-gather.19.cloned.1.call-done = bf16[2048,2048]{1,0:T(8,128)(2,1)} async-done(((bf16[256,2048]{1,0:T(8,128)(2,1)}), bf16[2048,2048]{1,0:T(8,128)(2,1)}) %all-gather.19.cloned.1.call-update) | async-done | bytes 8388624 | tf_op jit(solution)/shard_map/all_gather | solution.py:76
  1054.4 7.6 fusion.39
  1062.1 5.1 all-to-all-start.4
  1067.4 19.2 %convolution_convert_fusion.3 = bf16[2048,1536]{1,0:T(8,128)(2,1)} fusion(bf16[2048,2048]{1,0:T(8,128)(2,1)} %all-gather.13.cloned.1.call-done, bf16[2048,768]{0,1:T(8,128)(2,1)} %get-tuple-element.117, bf16[2048,768]{0,1:T(8,128)(2,1)} %copy-done.74), kind=kOutput, calls=%fused_computation.15 | convolution fusion | flops 12900630528 | bytes 20971520 | tf_op jit(solution)/shard_map/dot_general | solution.py:60
  1086.7 31.8 %all-to-all-done.4 = bf16[4,512,256]{2,1,0:T(8,128)(2,1)S(1)} async-done(((bf16[4,512,256]{2,1,0:T(8,128)(2,1)}), bf16[4,512,256]{2,1,0:T(8,128)(2,1)S(1)}, u32[]{:S(2)}, u32[]{:S(2)}) %all-to-all-start.4) | async-done | bytes 1048608 | tf_op jit(solution)/shard_map/all_to_all | solution.py:84
  1121.3 3.1 copy.299
  1126.4 21.9 %fusion.5 = bf16[2,2048,2048]{1,2,0:T(8,128)(2,1)} fusion(f32[2048,2048,2]{1,0,2:T(8,128)} %get-tuple-element.153, f32[2,2048]{1,0:T(2,128)S(1)} %fusion.41, f32[2,2048]{1,0:T(2,128)S(1)} %copy-done.57, pred[2048,2048]{0,1:T(8,128)(4,1)} %iota_compare_fusion, bf16[2048,2,128]{0,2,1:T(8,128)(2,1)S(1)} %copy.269, bf16[2048,512]{1,0:T(8,128)(2,1)} %bitcast.322), kind=kOutput, calls=%fused_computation.9 | convolution fusion | flops 2197815296 | bytes 56131584 | tf_op jit(solution)/shard_map/tkgd,skd->kgts/dot_general | solution.py:567
  1148.4 8.4 fusion.17
  1158.0 11.5 fusion.22
  1170.0 16.8 %fusion.21 = bf16[2048,1,128]{0,2,1:T(8,128)(2,1)S(1)} fusion(bf16[2048,2,128]{0,2,1:T(8,128)(2,1)} %copy-done.36, f32[2048,2048,2]{1,0,2:T(8,128)} %get-tuple-element.153, f32[2,2048]{1,0:T(2,128)S(1)} %copy-done.57, pred[2048,2048]{0,1:T(8,128)(4,1)} %iota_compare_fusion), kind=kOutput, calls=%fused_computation.52 | convolution fusion | flops 2181300224 | bytes 39337984 | tf_op jit(solution)/shard_map/kgts,tkgd->skd/dot_general | solution.py:579
  1188.7 6.5 all-to-all-start.5
  1195.4 6.7 convolution_convert_fusion.6
  1202.1 88.2 %all-to-all-done.5 = bf16[4,512,512]{1,2,0:T(8,128)(2,1)S(1)} async-done(((bf16[4,512,512]{1,2,0:T(8,128)(2,1)}), bf16[4,512,512]{1,2,0:T(8,128)(2,1)S(1)}, u32[]{:S(2)}, u32[]{:S(2)}) %all-to-all-start.5) | async-done | bytes 2097184 | tf_op jit(solution)/shard_map/all_to_all | solution.py:84
  1299.8 4.7 convolution_convert_fusion.5
  1310.2 3.4 reshape.462
  1313.6 4.7 multiply_reduce_fusion.2
  1318.7 12.7 fusion.43
  1331.4 11.7 add_convert_fusion
  1343.1 16.6 %all_to_all.62 = bf16[8,64,768]{2,1,0:T(8,128)(2,1)S(1)} all-to-all(bf16[8,64,768]{2,1,0:T(8,128)(2,1)} %bitcast.345), channel_id=1, replica_groups=mesh['dp'=4,'z'=4,'core'=2] {'dp','core'}, dimensions={0} | all-to-all | bytes 1572864 | tf_op jit(solution)/shard_map/all_to_all | solution.py:547
  1359.6 3.8 all-to-all-start.7
  1368.3 2.6 broadcast_in_dim_reshape.6
  1373.8 10.6 all-to-all-done.7
  1384.4 3.6 all-to-all-start.6
  1390.9 5.8 fusion.77
  1396.8 4.5 dynamic_update_slice.3
  1405.6 38.9 %reduce-scatter.14.cloned.1.call-done = bf16[256,2048]{1,0:T(8,128)(2,1)} async-done(((bf16[2048,2048]{1,0:T(8,128)(2,1)}), bf16[256,2048]{1,0:T(8,128)(2,1)}) %reduce-scatter.14.cloned.1.call-update) | async-done | bytes 1048592 | tf_op jit(solution)/shard_map/reduce_scatter | solution.py:80
  1448.3 3.5 fusion.28
  1451.8 2.7 reshape.472
  1456.3 3.0 broadcast_in_dim_reshape.7
  1459.4 113.2 %all-reduce.8.cloned.1.call-done = f32[37152]{0:T(1024)} async-done(((f32[37152]{0:T(1024)}), f32[37152]{0:T(1024)}) %all-reduce.8.cloned.1.call-update) | async-done | bytes 148624
  (331 shorter events, 110.4 us)
Async XLA Ops:
  8.0 8.9 copy-start.65
  8.0 9.1 copy-start.70
  8.0 9.1 copy-start.71
  8.0 9.1 copy-start.72
  8.1 9.1 copy-start.73
  10.1 20.3 %copy-start.27 = (bf16[1,256,2048]{2,1,0:T(8,128)(2,1)S(1)}, bf16[1,256,2048]{2,1,0:T(8,128)(2,1)}, u32[]{:S(2)}) copy-start(bf16[1,256,2048]{2,1,0:T(8,128)(2,1)} %param.16) | copy-start | bytes 3145732
  13.2 16.3 %all-to-all-start = ((bf16[8,64,768]{2,1,0:T(8,128)(2,1)}), bf16[8,64,768]{2,1,0:T(8,128)(2,1)S(1)}, u32[]{:S(2)}, u32[]{:S(2)}) async-start(bf16[8,64,768]{2,1,0:T(8,128)(2,1)} %copy.249), calls=%async_computation | async-start | bytes 1572864 | tf_op jit(solution)/shard_map/all_to_all | solution.py:464
  16.9 173.7 %all-reduce.6.cloned.1.call-start = ((), (), s32[]{:S(2)}) async-start(), calls=%async_computation.29 | async-start | bytes 151552
  18.2 218.4 %all-gather.11.cloned.1.call-start = ((), (), s32[]{:S(2)}) async-start(), calls=%async_computation.17 | async-start | bytes 3932160 | tf_op jit(solution)/shard_map/all_gather | solution.py:466
  30.4 217.1 %all-gather.9.cloned.1.call-start = ((), (), s32[]{:S(2)}) async-start(), calls=%async_computation.16 | async-start | bytes 9437184 | tf_op jit(solution)/shard_map/all_gather | solution.py:76
  36.2 461.9 %copy-start.2 = (f32[256,2048]{1,0:T(8,128)}, f32[256,2048]{1,0:T(8,128)S(1)}, u32[]{:S(2)}) copy-start(f32[256,2048]{1,0:T(8,128)S(1)} %reshape.477) | copy-start | bytes 6291460
  36.2 157.0 %copy-start.68 = (s32[1,256]{1,0:T(1,128)S(1)}, s32[1,256]{1,0:T(1,128)}, u32[]{:S(2)}) copy-start(s32[1,256]{1,0:T(1,128)} %param.18) | copy-start | bytes 3076
  36.2 157.6 %copy-start.69 = (s32[1,256]{1,0:T(1,128)S(1)}, s32[1,256]{1,0:T(1,128)}, u32[]{:S(2)}) copy-start(s32[1,256]{1,0:T(1,128)} %param.19) | copy-start | bytes 3076
  36.5 158.1 %copy-start.54 = (f32[256]{0:T(256)}, f32[256]{0:T(256)S(1)}, u32[]{:S(2)}) copy-start(f32[256]{0:T(256)S(1)} %add_rsqrt_fusion.3) | copy-start | bytes 3076
  190.5 45.5 %copy-start.45 = (bf16[37120]{0:T(1024)(128)(2,1)S(1)}, bf16[37120]{0:T(1024)(128)(2,1)}, u32[]{:S(2)}) copy-start(bf16[37120]{0:T(1024)(128)(2,1)} %all-reduce.6.cloned.1.call-done) | copy-start | bytes 222724
  193.8 803.2 %copy-start.58 = (f32[1,256]{1,0:T(1,128)}, f32[1,256]{1,0:T(1,128)S(1)}, u32[]{:S(2)}) copy-start(f32[1,256]{1,0:T(1,128)S(1)} %get-tuple-element.150) | copy-start | bytes 3076
  236.0 20.4 %copy-start.19 = (f32[2048,64]{0,1:T(8,128)}, f32[2048,64]{0,1:T(8,128)S(1)}, u32[]{:S(2)}) copy-start(f32[2048,64]{0,1:T(8,128)S(1)} %get-tuple-element.148) | copy-start | bytes 1572868
  236.0 20.4 %copy-start.25 = (f32[2048,64]{0,1:T(8,128)}, f32[2048,64]{0,1:T(8,128)S(1)}, u32[]{:S(2)}) copy-start(f32[2048,64]{0,1:T(8,128)S(1)} %get-tuple-element.149) | copy-start | bytes 1572868
  236.4 20.0 %copy-start.60 = (f32[128]{0:T(128)}, f32[128]{0:T(128)S(1)}, u32[]{:S(2)}) copy-start(f32[128]{0:T(128)S(1)} %reshape.480) | copy-start | bytes 1540
  236.5 19.2 %copy-start.62 = (f32[128]{0:T(128)}, f32[128]{0:T(128)S(1)}, u32[]{:S(2)}) copy-start(f32[128]{0:T(128)S(1)} %reshape.479) | copy-start | bytes 1540
  236.6 21.1 %copy-start.66 = (f32[256]{0:T(256)}, f32[256]{0:T(256)S(1)}, u32[]{:S(2)}) copy-start(f32[256]{0:T(256)S(1)} %broadcast_bitcast_fusion) | copy-start | bytes 3076
  260.3 51.2 %all-to-all-start.1 = ((bf16[4,512,512]{1,2,0:T(8,128)(2,1)}), bf16[4,512,512]{1,2,0:T(8,128)(2,1)}, u32[]{:S(2)}, u32[]{:S(2)}) async-start(bf16[4,512,512]{1,2,0:T(8,128)(2,1)} %pad_maximum_fusion.5), calls=%async_computation.1 | async-start | bytes 4194304 | tf_op jit(solution)/shard_map/all_to_all | solution.py:84
  319.4 16.4 %copy-start.28 = (bf16[2048,256]{0,1:T(8,128)(2,1)}, bf16[2048,256]{0,1:T(8,128)(2,1)S(1)}, u32[]{:S(2)}) copy-start(bf16[2048,256]{0,1:T(8,128)(2,1)S(1)} %copy.254) | copy-start | bytes 3145732
  319.4 16.4 %copy-start.11 = (pred[2048,2048]{0,1:T(8,128)(4,1)S(1)}, pred[2048,2048]{0,1:T(8,128)(4,1)}, u32[]{:S(2)}) copy-start(pred[2048,2048]{0,1:T(8,128)(4,1)} %iota_compare_fusion) | copy-start | bytes 12582916
  350.5 18.1 %copy-start.56 = (f32[2,2048]{1,0:T(2,128)}, f32[2,2048]{1,0:T(2,128)S(1)}, u32[]{:S(2)}) copy-start(f32[2,2048]{1,0:T(2,128)S(1)} %log_add_fusion) | copy-start | bytes 49156
  371.7 29.8 %all-to-all-start.2 = ((bf16[4,512,256]{1,2,0:T(8,128)(2,1)}), bf16[4,512,256]{1,2,0:T(8,128)(2,1)}, u32[]{:S(2)}, u32[]{:S(2)}) async-start(bf16[4,512,256]{1,2,0:T(8,128)(2,1)} %copy.258), calls=%async_computation.2 | async-start | bytes 2097152 | tf_op jit(solution)/shard_map/all_to_all | solution.py:84
  379.3 118.7 %reduce-scatter.8.cloned.1.call-start = ((), (), s32[]{:S(2)}) async-start(), calls=%async_computation.18 | async-start | bytes 9437184 | tf_op jit(solution)/shard_map/reduce_scatter | solution.py:80
  379.9 5.9 copy-start.23
  387.8 16.3 %copy-start.30 = (f32[2048,2]{1,0:T(8,128)S(1)}, f32[2048,2]{1,0:T(8,128)}, u32[]{:S(2)}) copy-start(f32[2048,2]{1,0:T(8,128)} %copy.260) | copy-start | bytes 49156
  404.1 6.0 copy-start.7
  418.3 245.1 %all-gather.15.cloned.1.call-start = ((), (), s32[]{:S(2)}) async-start(), calls=%async_computation.20 | async-start | bytes 11796480 | tf_op jit(solution)/shard_map/all_gather | solution.py:466
  461.1 260.3 %all-gather.13.cloned.1.call-start = ((), (), s32[]{:S(2)}) async-start(), calls=%async_computation.19 | async-start | bytes 9437184 | tf_op jit(solution)/shard_map/all_gather | solution.py:76
  502.2 325.4 %reduce-scatter.10.cloned.1.call-start = ((), (), s32[]{:S(2)}) async-start(), calls=%async_computation.21 | async-start | bytes 9437184 | tf_op jit(solution)/shard_map/reduce_scatter | solution.py:80
  739.1 4.5 copy-start.12
  756.3 129.1 %all-gather.17.cloned.1.call-start = ((), (), s32[]{:S(2)}) async-start(), calls=%async_computation.22 | async-start | bytes 9437184 | tf_op jit(solution)/shard_map/all_gather | solution.py:76
  761.3 66.3 %copy-start.5 = (f32[256,2048]{1,0:T(8,128)S(1)}, f32[256,2048]{1,0:T(8,128)}, u32[]{:S(2)}) copy-start(f32[256,2048]{1,0:T(8,128)} %copy-done.4) | copy-start | bytes 6291460
  831.1 162.1 %reduce-scatter.12.cloned.1.call-start = ((), (), s32[]{:S(2)}) async-start(), calls=%async_computation.23 | async-start | bytes 9437184 | tf_op jit(solution)/shard_map/reduce_scatter | solution.py:80
  921.9 71.3 %copy-start.15 = (bf16[256,2048]{1,0:T(8,128)(2,1)S(1)}, bf16[256,2048]{1,0:T(8,128)(2,1)}, u32[]{:S(2)}) copy-start(bf16[256,2048]{1,0:T(8,128)(2,1)} %reduce-scatter.10.cloned.1.call-done) | copy-start | bytes 3145732
  921.9 132.5 %all-gather.19.cloned.1.call-start = ((), (), s32[]{:S(2)}) async-start(), calls=%async_computation.24 | async-start | bytes 9437184 | tf_op jit(solution)/shard_map/all_gather | solution.py:76
  993.2 3.8 copy-start.6
  993.2 3.8 copy-start.32
  1000.1 343.0 %reduce-scatter.20.cloned.1.call-start = ((), (), s32[]{:S(2)}) async-start(), calls=%async_computation.28 | async-start | bytes 3932160 | tf_op jit(solution)/shard_map/reduce_scatter | solution.py:546
  1011.5 42.9 %copy-start.17 = (f32[2048,2,128]{2,1,0:T(2,128)S(1)}, f32[2048,2,128]{2,1,0:T(2,128)}, u32[]{:S(2)}) copy-start(f32[2048,2,128]{2,1,0:T(2,128)} %copy-done.16) | copy-start | bytes 6291460
  1062.1 56.4 %all-to-all-start.4 = ((bf16[4,512,256]{2,1,0:T(8,128)(2,1)}), bf16[4,512,256]{2,1,0:T(8,128)(2,1)S(1)}, u32[]{:S(2)}, u32[]{:S(2)}) async-start(bf16[4,512,256]{2,1,0:T(8,128)(2,1)} %bitcast.41), calls=%async_computation.7 | async-start | bytes 2097152 | tf_op jit(solution)/shard_map/all_to_all | solution.py:84
  1067.2 292.4 %reduce-scatter.18.cloned.1.call-start = ((), (), s32[]{:S(2)}) async-start(), calls=%async_computation.27 | async-start | bytes 7864320 | tf_op jit(solution)/shard_map/reduce_scatter | solution.py:546
  1121.3 5.1 copy-start.36
  1188.7 6.7 copy-start.22
  1188.7 101.6 %all-to-all-start.5 = ((bf16[4,512,512]{1,2,0:T(8,128)(2,1)}), bf16[4,512,512]{1,2,0:T(8,128)(2,1)S(1)}, u32[]{:S(2)}, u32[]{:S(2)}) async-start(bf16[4,512,512]{1,2,0:T(8,128)(2,1)} %pad_maximum_fusion.6), calls=%async_computation.8 | async-start | bytes 4194304 | tf_op jit(solution)/shard_map/all_to_all | solution.py:84
  1195.2 176.4 %reduce-scatter.16.cloned.1.call-start = ((), (), s32[]{:S(2)}) async-start(), calls=%async_computation.26 | async-start | bytes 3932160 | tf_op jit(solution)/shard_map/reduce_scatter | solution.py:546
  1290.6 8.4 copy-start.41
  1299.0 5.6 copy-start.42
  1299.8 4.8 copy-start.37
  1306.6 137.9 %reduce-scatter.14.cloned.1.call-start = ((), (), s32[]{:S(2)}) async-start(), calls=%async_computation.25 | async-start | bytes 9437184 | tf_op jit(solution)/shard_map/reduce_scatter | solution.py:80
  1318.7 12.7 copy-start.24
  1318.7 12.7 copy-start.50
  1359.6 24.8 %all-to-all-start.7 = ((bf16[8,64,1536]{2,1,0:T(8,128)(2,1)}), bf16[8,64,1536]{2,1,0:T(8,128)(2,1)S(1)}, u32[]{:S(2)}, u32[]{:S(2)}) async-start(bf16[8,64,1536]{2,1,0:T(8,128)(2,1)} %bitcast.336), calls=%async_computation.13 | async-start | bytes 3145728 | tf_op jit(solution)/shard_map/all_to_all | solution.py:547
  1365.0 5.9 copy-start.59
  1365.0 5.9 copy-start.64
  1384.4 17.9 %all-to-all-start.6 = ((bf16[8,64,768]{2,1,0:T(8,128)(2,1)}), bf16[8,64,768]{2,1,0:T(8,128)(2,1)S(1)}, u32[]{:S(2)}, u32[]{:S(2)}) async-start(bf16[8,64,768]{2,1,0:T(8,128)(2,1)} %bitcast.333), calls=%async_computation.11 | async-start | bytes 1572864 | tf_op jit(solution)/shard_map/all_to_all | solution.py:547
  1388.0 184.6 %all-reduce.8.cloned.1.call-start = ((), (), s32[]{:S(2)}) async-start(), calls=%async_computation.30 | async-start | bytes 303104
  1401.9 42.6 %copy-start.3 = (f32[256,2048]{1,0:T(8,128)S(1)}, f32[256,2048]{1,0:T(8,128)}, u32[]{:S(2)}) copy-start(f32[256,2048]{1,0:T(8,128)} %copy-done.2) | copy-start | bytes 6291460
  1401.9 42.6 %copy-start.52 = (f32[2048]{0:T(1024)S(1)}, f32[2048]{0:T(1024)}, u32[]{:S(2)}) copy-start(f32[2048]{0:T(1024)} %copy-done.51) | copy-start | bytes 24580
  1401.9 42.6 %copy-start.55 = (f32[256]{0:T(256)S(1)}, f32[256]{0:T(256)}, u32[]{:S(2)}) copy-start(f32[256]{0:T(256)} %copy-done.54) | copy-start | bytes 3076
  1444.5 3.8 copy-start.31
  (35 other events, 57.7 us)
Sparse Core Ops, SparseCore 0:
  23.9 166.6 all-reduce.5
  1448.4 124.1 all-reduce.7
Sparse Core Ops, SparseCore 1:
  30.5 60.5 all-gather.10
  193.2 54.1 all-gather.8
  418.4 79.6 reduce-scatter.7
  499.7 163.6 all-gather.14
  666.0 55.3 all-gather.12
  756.4 71.1 reduce-scatter.9
  831.2 54.2 all-gather.16
  922.0 71.1 reduce-scatter.11
  1000.2 54.2 all-gather.18
  1056.8 82.1 reduce-scatter.19
  1141.3 154.6 reduce-scatter.17
  1306.7 61.6 reduce-scatter.15
  1372.1 72.4 reduce-scatter.13

commit v2 on v1

--- a/solution.py
+++ b/solution.py
@@ -4,6 +4,8 @@
 import jax
 import jax.numpy as jnp
 from jax import lax
+from jax.experimental import pallas as pl
+from jax.experimental.pallas import tpu as pltpu
 from jax.sharding import Mesh
 from jax.sharding import PartitionSpec as P
 
@@ -72,16 +74,591 @@
     return jnp.dot(left, right, preferred_element_type=jnp.float32)
 
 
+MESH = pl.DeviceIdType.MESH
+HBM = pl.BlockSpec(memory_space=pltpu.HBM)
+VMEM = pl.BlockSpec(memory_space=pltpu.VMEM)
+STRIP = 16
+TILE = 128
+
+
+def place():
+    dp, z, core = lax.axis_index("dp"), lax.axis_index("z"), lax.axis_index("core")
+    across = dp + 1 - 2 * lax.rem(dp, 2)
+    along = dp + 2 - 4 * (dp // 2)
+    return dp, z, core, across, along, across + along - dp
+
+
+def meet(devices):
+    barrier = pltpu.get_barrier_semaphore()
+    for device in devices:
+        pl.semaphore_signal(barrier, inc=1, device_id=device, device_id_type=MESH)
+    pl.semaphore_wait(barrier, len(devices))
+
+
+def swap_tiles(values):
+    return jnp.concatenate(
+        [
+            values[:, TILE * (4 * (t % 4) + t // 4) : TILE * (4 * (t % 4) + t // 4 + 1)]
+            for t in range(16)
+        ],
+        axis=1,
+    )
+
+
+def spread(own, out, send, recv):
+    dp, z, core, across, along, corner = place()
+    half = own.shape[0] // 2
+    first, second = pl.ds(0, half), pl.ds(half, half)
+    x_side, y_side, twin = (across, z, core), (along, z, core), (dp, z, 1 - core)
+    mine, of_x, of_y, of_d = (2 * d + core for d in (dp, across, along, corner))
+
+    def copy(index, source, slot, part, device):
+        return pltpu.make_async_remote_copy(
+            src_ref=source,
+            dst_ref=out.at[slot, part],
+            send_sem=send.at[index],
+            recv_sem=recv.at[index],
+            device_id=device,
+            device_id_type=MESH,
+        )
+
+    copies = [
+        copy(0, own.at[first], mine, first, x_side),
+        copy(1, own.at[second], mine, second, x_side),
+        copy(2, own.at[second], mine, second, y_side),
+        copy(3, own.at[first], mine, first, y_side),
+        copy(4, out.at[of_x, first], of_x, first, y_side),
+        copy(5, out.at[of_y, second], of_y, second, x_side),
+        copy(6, own.at[first], mine, first, twin),
+        copy(7, own.at[second], mine, second, twin),
+        copy(8, out.at[of_x, first], of_x, first, twin),
+        copy(9, out.at[of_x, second], of_x, second, twin),
+        copy(10, out.at[of_y, first], of_y, first, twin),
+        copy(11, out.at[of_y, second], of_y, second, twin),
+        copy(12, out.at[of_d, first], of_d, first, twin),
+        copy(13, out.at[of_d, second], of_d, second, twin),
+    ]
+
+    def start_first():
+        for index in (0, 3, 6):
+            copies[index].start()
+
+    def start_second():
+        for index in (2, 1, 7):
+            copies[index].start()
+
+    def finish():
+        for arrived, onward in ((0, (4, 8)), (2, (5, 11)), (1, (9,)), (3, (10,)), (4, (12,)), (5, (13,))):
+            copies[arrived].wait_recv()
+            for index in onward:
+                copies[index].start()
+        for index in range(6, 14):
+            copies[index].wait_recv()
+        for each in copies:
+            each.wait_send()
+
+    return start_first, start_second, finish
+
+
+def gather_kernel(own, out, local, send, recv):
+    dp, z, core, across, along, corner = place()
+    meet([(across, z, core), (along, z, core), (dp, z, 1 - core)])
+    keep = pltpu.make_async_copy(own, out.at[2 * dp + core], local)
+    keep.start()
+    start_first, start_second, finish = spread(own, out, send, recv)
+    start_first()
+    start_second()
+    finish()
+    keep.wait()
+
+
 def plane_gather(rows):
-    return lax.all_gather(rows, PLANE, axis=0, tiled=True)
-
-
-def plane_sum(partial):
-    return lax.psum_scatter(partial, PLANE, scatter_dimension=0, tiled=True)
-
-
-def column_swap(values):
-    return lax.all_to_all(values, "z", 0, 0, tiled=True)
+    out = pl.pallas_call(
+        gather_kernel,
+        name="plane_gather",
+        out_shape=jax.ShapeDtypeStruct((8,) + rows.shape, rows.dtype),
+        in_specs=[HBM],
+        out_specs=HBM,
+        scratch_shapes=[
+            pltpu.SemaphoreType.DMA(()),
+            pltpu.SemaphoreType.DMA((14,)),
+            pltpu.SemaphoreType.DMA((14,)),
+        ],
+        compiler_params=pltpu.CompilerParams(has_side_effects=True, collective_id=0),
+        cost_estimate=pl.CostEstimate(flops=0, bytes_accessed=120 << 20, transcendentals=0),
+    )(rows)
+    return out.reshape(-1, rows.shape[1])
+
+
+def sum_kernel(tail, gathers, n_in, n_out, *refs):
+    partial, refs = refs[0], refs[1:]
+    ins, outs, refs = refs[:n_in], refs[n_in : n_in + n_out], refs[n_in + n_out :]
+    for out in outs:
+        if out.shape[0] == STRIP:
+            out[...] = jnp.zeros_like(out)
+    if gathers:
+        spread_out, refs = refs[0], refs[1:]
+        own, refs = refs[0], refs[1:]
+    held, twins, passed, load, send_a, recv_a, send_b, recv_b = refs[:8]
+    dp, z, core, across, along, corner = place()
+    meet([(across, z, core), (along, z, core), (dp, z, 1 - core)])
+    half = partial.shape[1] // 2
+    x_side, y_side, twin = (across, z, core), (along, z, core), (dp, z, 1 - core)
+    owners = (dp, across, along, corner)
+    order = [(3, 0), (3, 1), (1, 0), (2, 1), (2, 0), (1, 1), (0, 0), (0, 1)]
+    from_twin, from_own = {}, {}
+    for index, (owner, part) in enumerate(order):
+        rows = pl.ds(part * half, half)
+        from_twin[owner, part] = pltpu.make_async_remote_copy(
+            src_ref=partial.at[2 * owners[owner] + 1 - core, rows],
+            dst_ref=twins.at[owner, part],
+            send_sem=send_a.at[index],
+            recv_sem=recv_a.at[index],
+            device_id=twin,
+            device_id_type=MESH,
+        )
+        from_own[owner, part] = pltpu.make_async_copy(
+            partial.at[2 * owners[owner] + core, rows], held.at[owner, part], load.at[index]
+        )
+    for key in order:
+        from_twin[key].start()
+        from_own[key].start()
+
+    def arrive(owner, part):
+        from_twin[owner, part].wait_recv()
+        from_own[owner, part].wait()
+
+    def add(owner, part, others):
+        @pl.loop(0, half // STRIP)
+        def _(step):
+            rows = pl.ds(pl.multiple_of(step * STRIP, STRIP), STRIP)
+            total = held[owner, part, rows].astype(jnp.float32)
+            total = total + twins[owner, part, rows].astype(jnp.float32)
+            for other in others:
+                total = total + passed[other, rows].astype(jnp.float32)
+            held[owner, part, rows] = total.astype(jnp.bfloat16)
+
+    def last(part, others):
+        @pl.loop(0, half // STRIP)
+        def _(step):
+            rows = pl.ds(pl.multiple_of(step * STRIP, STRIP), STRIP)
+            total = held[0, part, rows].astype(jnp.float32)
+            total = total + twins[0, part, rows].astype(jnp.float32)
+            for other in others:
+                total = total + passed[other, rows].astype(jnp.float32)
+            rows = pl.ds(pl.multiple_of(part * half + step * STRIP, STRIP), STRIP)
+            sent = tail(rows, total, ins, outs)
+            if gathers:
+                own[rows] = sent
+
+    def pass_on(index, owner, part, device):
+        copy = pltpu.make_async_remote_copy(
+            src_ref=held.at[owner, part],
+            dst_ref=passed.at[index],
+            send_sem=send_b.at[index],
+            recv_sem=recv_b.at[index],
+            device_id=device,
+            device_id_type=MESH,
+        )
+        copy.start()
+        return copy
+
+    hops = []
+    for index, (owner, part, device) in enumerate(
+        [(3, 0, x_side), (3, 1, y_side), (1, 0, x_side), (2, 1, y_side)]
+    ):
+        arrive(owner, part)
+        add(owner, part, ())
+        hops.append(pass_on(index, owner, part, device))
+    arrive(2, 0)
+    hops[0].wait_recv()
+    add(2, 0, (0,))
+    hops.append(pass_on(4, 2, 0, y_side))
+    arrive(1, 1)
+    hops[1].wait_recv()
+    add(1, 1, (1,))
+    hops.append(pass_on(5, 1, 1, x_side))
+    arrive(0, 0)
+    arrive(0, 1)
+    hops[2].wait_recv()
+    hops[3].wait_recv()
+    if gathers:
+        keep = pltpu.make_async_copy(own, spread_out.at[2 * dp + core], refs[8])
+        start_first, start_second, finish = spread(own, spread_out, refs[9], refs[10])
+    hops[4].wait_recv()
+    last(0, (2, 4))
+    if gathers:
+        start_first()
+    hops[5].wait_recv()
+    last(1, (3, 5))
+    if gathers:
+        start_second()
+        keep.start()
+        finish()
+        keep.wait()
+    for key in order:
+        from_twin[key].wait_send()
+    for hop in hops:
+        hop.wait_send()
+
+
+def plane_sum(name, number, tail, partial, ins, outs, gathers):
+    width = partial.shape[1]
+    partial = partial.reshape(8, -1, width)
+    rows = partial.shape[1]
+    half = rows // 2
+    out_shape = [jax.ShapeDtypeStruct(shape, dtype) for shape, dtype in outs]
+    out_specs = [VMEM] * len(outs)
+    scratch = [
+        pltpu.VMEM((4, 2, half, width), jnp.bfloat16),
+        pltpu.VMEM((4, 2, half, width), jnp.bfloat16),
+        pltpu.VMEM((6, half, width), jnp.bfloat16),
+        pltpu.SemaphoreType.DMA((8,)),
+        pltpu.SemaphoreType.DMA((8,)),
+        pltpu.SemaphoreType.DMA((8,)),
+        pltpu.SemaphoreType.DMA((6,)),
+        pltpu.SemaphoreType.DMA((6,)),
+    ]
+    if gathers:
+        out_shape.append(jax.ShapeDtypeStruct((8, rows, width), jnp.bfloat16))
+        out_specs.append(HBM)
+        scratch = (
+            [pltpu.VMEM((rows, width), jnp.bfloat16)]
+            + scratch
+            + [
+                pltpu.SemaphoreType.DMA(()),
+                pltpu.SemaphoreType.DMA((14,)),
+                pltpu.SemaphoreType.DMA((14,)),
+            ]
+        )
+    results = pl.pallas_call(
+        functools.partial(sum_kernel, tail, gathers, len(ins), len(outs)),
+        name=name,
+        out_shape=out_shape,
+        in_specs=[HBM] + [VMEM] * len(ins),
+        out_specs=out_specs,
+        scratch_shapes=scratch,
+        compiler_params=pltpu.CompilerParams(
+            has_side_effects=True, collective_id=number, vmem_limit_bytes=48 << 20
+        ),
+        cost_estimate=pl.CostEstimate(flops=0, bytes_accessed=240 << 20, transcendentals=0),
+    )(partial, *ins)
+    if gathers:
+        results = list(results[:-1]) + [results[-1].reshape(-1, width)]
+    return results
+
+
+def middle_tail(rows, total, ins, outs):
+    hidden, gain = ins
+    (middle,) = outs
+    mid = swap_tiles(hidden[rows]).astype(jnp.float32) + total
+    middle[rows] = mid
+    return (normalize(mid) * gain[...]).astype(jnp.bfloat16)
+
+
+def result_tail(rows, total, ins, outs):
+    middle, targets, counted, weight = ins
+    result, d_result, error = outs
+
+    value = middle[rows] + total
+    result[rows] = swap_tiles(value.astype(jnp.bfloat16))
+    difference = value - swap_tiles(targets[rows]).astype(jnp.float32)
+    error[...] += counted[rows] * (difference * difference)
+    grad = weight[rows] * difference
+    d_result[rows] = grad
+    return grad.astype(jnp.bfloat16)
+
+
+def middle_back_tail(rows, total, ins, outs):
+    middle, gain, d_result = ins
+    d_middle, grad_gain = outs
+    mid = middle[rows]
+    factor = lax.rsqrt(jnp.mean(mid * mid, axis=-1, keepdims=True) + EPSILON)
+    unit = mid * factor
+    grad_gain[...] += total * unit
+    grad = total * gain[...]
+    back = factor * (grad - unit * jnp.mean(grad * unit, axis=-1, keepdims=True))
+    back = d_result[rows] + back
+    d_middle[rows] = back
+    return back.astype(jnp.bfloat16)
+
+
+def inputs_back_tail(rows, total, ins, outs):
+    hidden, gain, d_middle = ins
+    grad_inputs, grad_gain = outs
+    values = swap_tiles(hidden[rows]).astype(jnp.float32)
+    factor = lax.rsqrt(jnp.mean(values * values, axis=-1, keepdims=True) + EPSILON)
+    unit = values * factor
+    grad_gain[...] += total * unit
+    grad = total * gain[...]
+    back = factor * (grad - unit * jnp.mean(grad * unit, axis=-1, keepdims=True))
+    grad_inputs[rows] = swap_tiles(d_middle[rows] + back)
+
+
+Q_BLOCK = 256
+
+
+def column_copies(sent, landed, send, recv, local):
+    dp, z, core = lax.axis_index("dp"), lax.axis_index("z"), lax.axis_index("core")
+
+    def start(to):
+        @pl.when(to != z)
+        def _():
+            pltpu.make_async_remote_copy(
+                src_ref=sent.at[to],
+                dst_ref=landed.at[z],
+                send_sem=send.at[to],
+                recv_sem=recv.at[z],
+                device_id=(dp, to, core),
+                device_id_type=MESH,
+            ).start()
+
+        @pl.when(to == z)
+        def _():
+            pltpu.make_async_copy(sent.at[to], landed.at[to], local).start()
+
+    def await_arrival(source):
+        @pl.when(source != z)
+        def _():
+            pltpu.make_async_remote_copy(
+                src_ref=sent.at[source],
+                dst_ref=landed.at[source],
+                send_sem=send.at[source],
+                recv_sem=recv.at[source],
+                device_id=(dp, source, core),
+                device_id_type=MESH,
+            ).wait_recv()
+
+        @pl.when(source == z)
+        def _():
+            pltpu.make_async_copy(sent.at[source], landed.at[source], local).wait()
+
+    def await_sent(to):
+        @pl.when(to != z)
+        def _():
+            pltpu.make_async_remote_copy(
+                src_ref=sent.at[to],
+                dst_ref=landed.at[z],
+                send_sem=send.at[to],
+                recv_sem=recv.at[z],
+                device_id=(dp, to, core),
+                device_id_type=MESH,
+            ).wait_send()
+
+    return start, await_arrival, await_sent
+
+
+def meet_column():
+    dp, z, core = lax.axis_index("dp"), lax.axis_index("z"), lax.axis_index("core")
+    meet([(dp, lax.rem(z + step, 4), core) for step in (1, 2, 3)])
+
+
+def head_lanes(head):
+    return pl.ds(pl.multiple_of(head * HD, HD), HD)
+
+
+def causal_scores(keys, queries, start):
+    scores = lax.dot_general(
+        keys, queries, (((1,), (1,)), ((), ())), preferred_element_type=jnp.float32
+    )
+    key_at = lax.broadcasted_iota(jnp.int32, (Q_BLOCK, Q_BLOCK), 0)
+    query_at = lax.broadcasted_iota(jnp.int32, (Q_BLOCK, Q_BLOCK), 1)
+    edge = jnp.where(key_at <= query_at, scores[start:], MASKED)
+    return edge if start == 0 else jnp.concatenate([scores[:start], edge], axis=0)
+
+
+def attend_kernel(
+    exponent, sent, back, held, attended, log_total, mixed, flipped, send, recv, sent_b, recv_b, local
+):
+    meet_column()
+    start, await_arrival, await_sent = column_copies(sent, held, send, recv, local.at[0])
+    start_b, await_arrival_b, await_sent_b = column_copies(mixed, back, sent_b, recv_b, local.at[1])
+    for block in range(4):
+        start(block)
+    for block in range(4):
+        await_arrival(block)
+    chunk = held.shape[1]
+    tokens = 4 * chunk
+    q_cols = mixed.shape[2]
+    for block in range(4):
+        flipped[:, chunk * block : chunk * (block + 1)] = held[block, :, q_cols + HD :].T
+    per = chunk // Q_BLOCK
+    for block in range(tokens // Q_BLOCK):
+        first = block * Q_BLOCK
+        limit = first + Q_BLOCK
+
+        @pl.loop(0, q_cols // HD)
+        def _(head):
+            queries = held[block // per, pl.ds((block % per) * Q_BLOCK, Q_BLOCK), head_lanes(head)]
+            keys = jnp.concatenate(
+                [
+                    held[b, : min(chunk, limit - b * chunk), q_cols : q_cols + HD]
+                    for b in range(-(-limit // chunk))
+                ],
+                axis=0,
+            )
+            scores = causal_scores(keys, queries, first)
+            highest = jnp.max(scores, axis=0, keepdims=True)
+            weights = jnp.exp2((scores - highest) * exponent)
+            total = jnp.sum(weights, axis=0, keepdims=True)
+            mix = jnp.dot(
+                flipped[:, :limit],
+                weights.astype(jnp.bfloat16),
+                preferred_element_type=jnp.float32,
+            )
+            mix = (mix / total).T
+            attended[pl.ds(first, Q_BLOCK), head_lanes(head)] = mix
+            mixed[block // per, pl.ds((block % per) * Q_BLOCK, Q_BLOCK), head_lanes(head)] = (
+                mix.astype(jnp.bfloat16)
+            )
+            log_total[head, :, pl.ds(first, Q_BLOCK)] = highest * exponent + jnp.log2(total)
+
+        if (block + 1) % per == 0:
+            start_b(block // per)
+    for block in range(4):
+        await_arrival_b(block)
+    for block in range(4):
+        await_sent(block)
+        await_sent_b(block)
+
+
+def attend_back_kernel(
+    exponent,
+    sent,
+    held,
+    attended,
+    log_total,
+    back,
+    landed,
+    d_held,
+    flipped,
+    d_keys,
+    d_values,
+    send,
+    recv,
+    sent_b,
+    recv_b,
+    local,
+):
+    meet_column()
+    start, await_arrival, await_sent = column_copies(sent, landed, send, recv, local.at[0])
+    start_b, await_arrival_b, await_sent_b = column_copies(d_held, back, sent_b, recv_b, local.at[1])
+    for block in range(4):
+        start(block)
+    chunk = held.shape[1]
+    tokens = 4 * chunk
+    q_cols = landed.shape[2]
+    for block in range(4):
+        flipped[:, chunk * block : chunk * (block + 1)] = held[block, :, q_cols : q_cols + HD].T
+    d_keys[...] = jnp.zeros_like(d_keys)
+    d_values[...] = jnp.zeros_like(d_values)
+    scale = HD ** (-0.5)
+    for block in range(4):
+        await_arrival(block)
+    per = chunk // Q_BLOCK
+    for block in reversed(range(tokens // Q_BLOCK)):
+        first = block * Q_BLOCK
+        limit = first + Q_BLOCK
+        rows = pl.ds((block % per) * Q_BLOCK, Q_BLOCK)
+
+        def upto(lanes):
+            return jnp.concatenate(
+                [
+                    held[b, : min(chunk, limit - b * chunk), lanes]
+                    for b in range(-(-limit // chunk))
+                ],
+                axis=0,
+            )
+
+        @pl.loop(0, q_cols // HD)
+        def _(head):
+            queries = held[block // per, rows, head_lanes(head)]
+            d_mix = landed[block // per, rows, head_lanes(head)]
+            scores = causal_scores(upto(slice(q_cols, q_cols + HD)), queries, first)
+            weights = jnp.exp2(scores * exponent - log_total[head, :, pl.ds(first, Q_BLOCK)])
+            product = d_mix.astype(jnp.float32) * attended[pl.ds(first, Q_BLOCK), head_lanes(head)]
+            row_dot = jnp.sum(product.T, axis=0, keepdims=True)
+            d_weights = lax.dot_general(
+                upto(slice(q_cols + HD, q_cols + 2 * HD)),
+                d_mix,
+                (((1,), (1,)), ((), ())),
+                preferred_element_type=jnp.float32,
+            )
+            d_scores = (weights * (d_weights - row_dot)).astype(jnp.bfloat16)
+            d_values[:limit] += jnp.dot(
+                weights.astype(jnp.bfloat16), d_mix, preferred_element_type=jnp.float32
+            )
+            d_keys[:limit] += jnp.dot(d_scores, queries, preferred_element_type=jnp.float32)
+            d_queries = jnp.dot(flipped[:, :limit], d_scores, preferred_element_type=jnp.float32)
+            d_held[block // per, rows, head_lanes(head)] = (d_queries.T * scale).astype(
+                jnp.bfloat16
+            )
+
+        if block % per == 0:
+            part = block // per
+            whole = pl.ds(first, chunk)
+            d_held[part, :, q_cols : q_cols + HD] = (d_keys[whole] * scale).astype(jnp.bfloat16)
+            d_held[part, :, q_cols + HD :] = d_values[whole].astype(jnp.bfloat16)
+            start_b(part)
+    for block in range(4):
+        await_arrival_b(block)
+    for block in range(4):
+        await_sent(block)
+        await_sent_b(block)
+
+
+EXPONENT = HD ** (-0.5) * math.log2(math.e)
+COLUMN_SEMAPHORES = [pltpu.SemaphoreType.DMA((4,))] * 4 + [pltpu.SemaphoreType.DMA((2,))]
+
+
+def attend_sequence(sent):
+    _, chunk, cols = sent.shape
+    q_cols = cols - 2 * HD
+    return pl.pallas_call(
+        functools.partial(attend_kernel, EXPONENT),
+        name="attend_sequence",
+        out_shape=[
+            jax.ShapeDtypeStruct((4, chunk, q_cols), jnp.bfloat16),
+            jax.ShapeDtypeStruct((4, chunk, cols), jnp.bfloat16),
+            jax.ShapeDtypeStruct((4 * chunk, q_cols), jnp.float32),
+            jax.ShapeDtypeStruct((q_cols // HD, 1, 4 * chunk), jnp.float32),
+        ],
+        in_specs=[HBM],
+        out_specs=[HBM, VMEM, VMEM, VMEM],
+        scratch_shapes=[
+            pltpu.VMEM((4, chunk, q_cols), jnp.bfloat16),
+            pltpu.VMEM((HD, 4 * chunk), jnp.bfloat16),
+        ]
+        + COLUMN_SEMAPHORES,
+        compiler_params=pltpu.CompilerParams(
+            has_side_effects=True, collective_id=5, vmem_limit_bytes=48 << 20
+        ),
+        cost_estimate=pl.CostEstimate(flops=0, bytes_accessed=240 << 20, transcendentals=0),
+    )(sent)
+
+
+def attend_sequence_back(sent, held, attended, log_total):
+    _, chunk, cols = held.shape
+    q_cols = cols - 2 * HD
+    return pl.pallas_call(
+        functools.partial(attend_back_kernel, EXPONENT),
+        name="attend_sequence_back",
+        out_shape=jax.ShapeDtypeStruct((4, chunk, cols), jnp.bfloat16),
+        in_specs=[HBM, VMEM, VMEM, VMEM],
+        out_specs=HBM,
+        scratch_shapes=[
+            pltpu.VMEM((4, chunk, q_cols), jnp.bfloat16),
+            pltpu.VMEM((4, chunk, cols), jnp.bfloat16),
+            pltpu.VMEM((HD, 4 * chunk), jnp.bfloat16),
+            pltpu.VMEM((4 * chunk, HD), jnp.float32),
+            pltpu.VMEM((4 * chunk, HD), jnp.float32),
+        ]
+        + COLUMN_SEMAPHORES,
+        compiler_params=pltpu.CompilerParams(
+            has_side_effects=True, collective_id=6, vmem_limit_bytes=48 << 20
+        ),
+        cost_estimate=pl.CostEstimate(flops=0, bytes_accessed=300 << 20, transcendentals=0),
+    )(sent, held, attended, log_total)
 
 
 def block_scores(queries, keys_all, values_all, first_row, step_index, key_block):
@@ -427,11 +1004,6 @@
         blocks = values.reshape(lead + (dp_n, z_n, 2 * piece))
         return jnp.swapaxes(blocks, -3, -2).reshape(lead + (width,))
 
-    def to_outer(values):
-        lead = values.shape[:-1]
-        blocks = values.reshape(lead + (z_n, dp_n, 2 * piece))
-        return jnp.swapaxes(blocks, -3, -2).reshape(lead + (width,))
-
     whole_parts = jnp.concatenate([positions[0], jnp.sum(valid[0])[None].astype(jnp.int32)])
     whole_all = lax.all_gather(whole_parts, EVERY, axis=0).reshape(dp_n, z_n, 2, rows_here + 1)
     valid_count = jnp.sum(whole_all[..., -1]).astype(jnp.float32)
@@ -493,54 +1065,58 @@
         ],
         axis=1,
     )
-    held = column_swap(sent)
-    queries = held[:, :q_cols].reshape(tokens, group, q_heads // group, HD)
-    keys = held[:, q_cols : q_cols + k_cols].reshape(tokens, group, HD)
-    values = held[:, q_cols + k_cols :].reshape(tokens, group, HD)
-    causal = lax.iota(jnp.int32, tokens)[None, :] <= lax.iota(jnp.int32, tokens)[:, None]
-    score_scale = HD ** (-0.5)
-    scores = (
-        jnp.einsum("tkgd,skd->kgts", queries, keys, preferred_element_type=jnp.float32)
-        * score_scale
-    )
-    scores = jnp.where(causal, scores, MASKED)
-    log_total = jax.nn.logsumexp(scores, axis=-1)
-    probs = jnp.exp(scores - log_total[..., None])
-    attended = jnp.einsum(
-        "kgts,skd->tkgd", probs.astype(jnp.bfloat16), values, preferred_element_type=jnp.float32
-    )
-    attended_back = column_swap(attended.astype(jnp.bfloat16).reshape(tokens, q_cols))
+    attended_back, held, attended, log_total = attend_sequence(sent.reshape(dp_n, -1, sent.shape[1]))
     attended_heads = attended_back.reshape(tokens, q_heads, HD).astype(jnp.float32)
     gate_open = jax.nn.sigmoid(gate_logit)
     gated = (attended_heads * gate_open[:, :, None]).reshape(tokens, q_cols).astype(jnp.bfloat16)
-    branch = plane_sum(contract_cols(gated, w_out_t).astype(jnp.bfloat16))
-    middle = hidden_in + branch.astype(jnp.float32)
-    unit_mid = normalize(middle)
-    normed_mid = plane_gather((unit_mid * gain_two).astype(jnp.bfloat16))
+    partial = contract_cols(gated, w_out_t).astype(jnp.bfloat16)
+    middle, normed_mid = plane_sum(
+        "middle_sum",
+        1,
+        middle_tail,
+        partial,
+        (inputs[0], gain_two[None]),
+        [((rows_here, width), jnp.float32)],
+        True,
+    )
     gate_up = matmul(normed_mid, w_gate_up)
     gate_pre, up_proj = gate_up[:, :ff_cols], gate_up[:, ff_cols:]
     sigmoid_gate = jax.nn.sigmoid(gate_pre)
     activated = (gate_pre * sigmoid_gate * up_proj).astype(jnp.bfloat16)
-    branch = plane_sum(contract_cols(activated, w_down_t).astype(jnp.bfloat16))
-    result = middle + branch.astype(jnp.float32)
-
-    weight_rows = valid[0].astype(jnp.float32)
-    difference = result - to_inner(targets[0]).astype(jnp.float32)
-    error_local = jnp.sum(weight_rows * jnp.mean(difference * difference, axis=-1))
+    partial = contract_cols(activated, w_down_t).astype(jnp.bfloat16)
+    counted = valid[0].astype(jnp.float32)[:, None]
     tokens_all = dp_n * z_n * 2 * rows_here
-    d_result = weight_rows[:, None] * difference * (tokens_all / valid_count)
-    d_branch = plane_gather(d_result.astype(jnp.bfloat16))
+    result, d_result, error_sums, d_branch = plane_sum(
+        "result_sum",
+        2,
+        result_tail,
+        partial,
+        (middle, targets[0], counted, counted * (tokens_all / valid_count)),
+        [
+            ((rows_here, width), jnp.bfloat16),
+            ((rows_here, width), jnp.float32),
+            ((STRIP, width), jnp.float32),
+        ],
+        True,
+    )
+    error_local = jnp.sum(error_sums) / width
     d_activated = matmul(d_branch, w_down_t)
     grad_down_t = contract_rows(d_branch, activated).astype(jnp.bfloat16)
     d_gate = d_activated * up_proj * sigmoid_gate * (1.0 + gate_pre * (1.0 - sigmoid_gate))
     d_up = d_activated * gate_pre * sigmoid_gate
     d_gate_up = jnp.concatenate([d_gate, d_up], axis=1).astype(jnp.bfloat16)
     grad_gate_up = contract_rows(normed_mid, d_gate_up).astype(jnp.bfloat16)
-    d_normed_mid = plane_sum(contract_cols(d_gate_up, w_gate_up).astype(jnp.bfloat16)).astype(
-        jnp.float32
-    )
-    grad_gain_two = jnp.sum(d_normed_mid * unit_mid, axis=0)
-    d_middle = d_result + norm_back(d_normed_mid * gain_two, middle)
+    partial = contract_cols(d_gate_up, w_gate_up).astype(jnp.bfloat16)
+    d_middle, gain_two_sums, d_attn = plane_sum(
+        "middle_back_sum",
+        3,
+        middle_back_tail,
+        partial,
+        (middle, gain_two[None], d_result),
+        [((rows_here, width), jnp.float32), ((STRIP, width), jnp.float32)],
+        True,
+    )
+    grad_gain_two = jnp.sum(gain_two_sums, axis=0)
 
     def settle(grads):
         summed = lax.psum_scatter(grads, "z", scatter_dimension=0, tiled=True)
@@ -555,42 +1131,15 @@
     gate_up_own = settle(grad_gate_up)
     down_own = settle(grad_down_t)
 
-    d_attn = plane_gather(d_middle.astype(jnp.bfloat16))
     d_gated = matmul(d_attn, w_out_t).reshape(tokens, q_heads, HD)
     grad_out_t = contract_rows(d_attn, gated).astype(jnp.bfloat16)
     d_attended = (d_gated * gate_open[:, :, None]).astype(jnp.bfloat16)
     d_gate_logit = (
         jnp.sum(d_gated * attended_heads, axis=-1) * gate_open * (1.0 - gate_open)
     ).astype(jnp.bfloat16)
-    d_attended = column_swap(d_attended.reshape(tokens, q_cols)).reshape(queries.shape)
-    row_dot = jnp.einsum("tkgd,tkgd->kgt", d_attended.astype(jnp.float32), attended)
-    d_probs = jnp.einsum(
-        "tkgd,skd->kgts", d_attended, values, preferred_element_type=jnp.float32
-    )
-    d_scores = (probs * (d_probs - row_dot[..., None])).astype(jnp.bfloat16)
-    d_queries = (
-        jnp.einsum("kgts,skd->tkgd", d_scores, keys, preferred_element_type=jnp.float32)
-        * score_scale
-    )
-    d_keys = (
-        jnp.einsum("kgts,tkgd->skd", d_scores, queries, preferred_element_type=jnp.float32)
-        * score_scale
-    )
-    d_values = jnp.einsum(
-        "kgts,tkgd->skd",
-        probs.astype(jnp.bfloat16),
-        d_attended,
-        preferred_element_type=jnp.float32,
-    )
-    sent = jnp.concatenate(
-        [
-            d_queries.reshape(tokens, q_cols),
-            d_keys.reshape(tokens, k_cols),
-            d_values.reshape(tokens, k_cols),
-        ],
-        axis=1,
-    ).astype(jnp.bfloat16)
-    held = column_swap(sent)
+    held = attend_sequence_back(
+        d_attended.reshape(dp_n, -1, q_cols), held, attended, log_total
+    ).reshape(tokens, -1)
     d_query_rot = rope_back(
         held[:, :q_cols].reshape(tokens, q_heads, HD).astype(jnp.float32), cosine, sine
     )
@@ -615,9 +1164,16 @@
     grad_logit = contract_rows(normed_all, d_gate_logit)
     attn_own = settle(jnp.concatenate([grad_qkv, grad_out_t], axis=1))
     d_normed_in = contract_cols(d_qkv, w_qkv) + contract_cols(d_gate_logit, w_logit)
-    d_normed_in = plane_sum(d_normed_in.astype(jnp.bfloat16)).astype(jnp.float32)
-    grad_gain_one = jnp.sum(d_normed_in * unit_in, axis=0)
-    grad_inputs = d_middle + norm_back(d_normed_in * gain_one, hidden_in)
+    grad_inputs, gain_one_sums = plane_sum(
+        "inputs_back_sum",
+        4,
+        inputs_back_tail,
+        d_normed_in.astype(jnp.bfloat16),
+        (inputs[0], gain_one[None], d_middle),
+        [((rows_here, width), jnp.float32), ((STRIP, width), jnp.float32)],
+        False,
+    )
+    grad_gain_one = jnp.sum(gain_one_sums, axis=0)
 
     devices = dp_n * z_n * 2
     logit_wide = lax.dynamic_update_slice(
@@ -641,9 +1197,9 @@
     small_own = lax.psum_scatter(small_sums.reshape(-1), EVERY, scatter_dimension=0, tiled=True)
     loss = small_own[-1] / valid_count
     return (
-        to_outer(result.astype(jnp.bfloat16))[None],
+        result[None],
         loss,
-        to_outer(grad_inputs)[None],
+        grad_inputs[None],
         small_own[:piece],
         take(attn_own, 0, q_cols),
         take(attn_own, q_cols, k_cols),
@@ -661,7 +1217,7 @@
 
 def solution(mesh):
     dp_n, ctx_n = mesh.shape["dp"], mesh.shape["ctx"]
-    split = ctx_n == 2 * dp_n and KV % (2 * dp_n) == 0
+    split = dp_n == 4 and ctx_n == 8
     if split:
         mesh = Mesh(mesh.devices.reshape(dp_n, ctx_n // 2, 2), EVERY)
         on_device = functools.partial(tensor_parallel, dp_n, ctx_n // 2)

time: 1590 us -> 1390 us (0.87)
  waiting for transfers between devices: 1000 us -> 502 us
  Pallas kernels: 0 us -> 489 us
  matrix products: 257 us -> 162 us
  other arithmetic: 66.3 us -> 29 us
  blocking collectives: 95.4 us -> 73 us
  starting transfers between devices: 38.1 us -> 16.5 us
  local copies, waits for them, and re-layouts: 111 us -> 93.1 us
    pallas_call x0 -> x7, Pallas kernels: none -> 489 us  [the longest x4 303 us: plane_sum(): pl.pallas_call(functools.partial(sum_kernel, tail, gathers, len(ins), len...]
    reduce_scatter x4 -> x0, waiting for transfers between devices: 209 us -> none  [plane_sum(): return lax.psum_scatter(partial, PLANE, scatter_dimension=0, tiled=True)]
    all_to_all x4 -> x0, waiting for transfers between devices: 175 us -> none  [column_swap(): return lax.all_to_all(values, 'z', 0, 0, tiled=True)]
    all_gather x4 -> x0, waiting for transfers between devices: 166 us -> none  [plane_gather(): return lax.all_gather(rows, PLANE, axis=0, tiled=True)]
    all_gather x2, waiting for transfers between devices: 161 us -> 0.03 us  [assemble(): return lax.all_gather(mine, 'z', axis=0, tiled=True)]
    reduce_scatter x3, waiting for transfers between devices: 0.03 us -> 153 us  [settle(): summed = lax.psum_scatter(grads, 'z', scatter_dimension=0, tiled=True)]
    dot_general x6 -> x0, matrix products: 93.1 us -> none  [the longest x1 21.9 us: tensor_parallel(): jnp.einsum('tkgd,skd->kgts', d_attended, values, preferred_element_type=j...]
    unnamed x17 -> x9, waiting for transfers between devices: 268 us -> 338 us
  transfers between devices with their start and end apart: 22 -> 11, of which waited for: 17 -> 6; matrix products, arithmetic and copies ran while one was open for 15% -> 11% of each run, Pallas kernels for 0% -> 18%
where the time goes in v2:
time: 1390 us
  waiting for transfers between devices  502 us (36%)
  Pallas kernels  489 us (35%)
  matrix products  162 us (12%)
  local copies, waits for them, and re-layouts  93.1 us (7%)
  blocking collectives  73 us (5%)
  other arithmetic  29 us (2%)
  between operations  20.3 us (1%)
  starting transfers between devices  16.5 us (1%)
    unnamed x9, waiting for transfers between devices  338 us
    pallas_call x4, Pallas kernels, plane_sum(): pl.pallas_call(functools.partial(sum_kernel, tail, gathers, len(ins), len...  303 us
    reduce_scatter x3, waiting for transfers between devices, settle(): summed = lax.psum_scatter(grads, 'z', scatter_dimension=0, tiled=True)  153 us
    pallas_call x1, Pallas kernels, attend_sequence_back(): pl.pallas_call(functools.partial(attend_back_kernel, EXPONENT), name='att...  75.2 us
    pallas_call x1, Pallas kernels, attend_sequence(): pl.pallas_call(functools.partial(attend_kernel, EXPONENT), name='attend_s...  71.9 us
    dot_general x5, matrix products, contract_cols(): lax.dot_general(left, right, (((1,), (1,)), ((), ())), preferred_element_...  62.6 us
    dot_general x5, matrix products, matmul(): return jnp.dot(left, right, preferred_element_type=jnp.float32)  55.6 us
    dot_general x5, matrix products, contract_rows(): lax.dot_general(left, right, (((0,), (0,)), ((), ())), preferred_element_...  43.8 us
  transfers between devices with their start and end apart: 11, of which 6 were waited for; matrix products, arithmetic and copies ran while one was open for 11% of the time, Pallas kernels for 18%

profile of v2, /device:TPU:8, one launch (start us, length us, event | category | flops | bytes accessed | tf_op | source)
XLA Modules:
  0.0 1385.8 jit_solution(10073510998216279322)
XLA Ops:
  13.2 3.9 all-to-all-start
  18.4 11.2 all-to-all-done
  31.6 32.8 %all_to_all.25 = bf16[8,64,2304]{2,1,0:T(8,128)(2,1)} all-to-all(bf16[8,64,2304]{2,1,0:T(8,128)(2,1)S(1)} %copy.205), channel_id=1, replica_groups=mesh['dp'=4,'z'=4,'core'=2] {'dp','core'}, dimensions={0} | all-to-all | bytes 4718592 | tf_op jit(solution)/shard_map/all_to_all | solution.py:1036
  64.5 1.7 reshape.428
  66.3 1.9 copy.254
  68.1 2.1 reshape.412
  71.7 40.2 %all-reduce.1 = s32[8224]{0:T(1024)S(1)} all-reduce(s32[8224]{0:T(1024)S(1)} %add_dynamic-update-slice_fusion), channel_id=3, replica_groups=mesh['dp'=4,'z'=4,'core'=2] {'dp','z','core'}, use_global_device_ids=true, to_apply=%add.1 | all-reduce | flops 8224 | bytes 65792
  114.0 2.8 multiply_cosine_fusion
  116.8 213.1 %all-reduce.6.cloned.1.call-done = bf16[37120]{0:T(1024)(128)(2,1)} async-done(((bf16[37120]{0:T(1024)(128)(2,1)}), bf16[37120]{0:T(1024)(128)(2,1)}) %all-reduce.6.cloned.1.call-update) | async-done | bytes 74256
  334.5 39.8 %plane_gather.1 = bf16[8,256,2048]{2,1,0:T(8,128)(2,1)} custom-call(bf16[256,2048]{1,0:T(8,128)(2,1)} %multiply_convert_fusion.5.own), custom_call_target="tpu_custom_call" | custom-call | bytes 125829120 | tf_op jit(solution)/shard_map/plane_gather/pallas_call | solution.py:176
  376.0 5.7 fusion.8
  382.6 1.8 copy.204
  384.5 7.6 fusion.17
  395.4 1.3 pad_maximum_fusion.8
  401.7 1.5 pad_maximum_fusion.5.sent
  403.2 71.9 %attend_sequence.1 = (bf16[4,512,256]{2,1,0:T(8,128)(2,1)S(1)}, bf16[4,512,512]{2,1,0:T(8,128)(2,1)S(1)}, f32[2048,256]{1,0:T(8,128)S(1)}, f32[2,1,2048]{2,1,0:T(1,128)S(1)}) custom-call(bf16[4,512,512]{2,1,0:T(8,128)(2,1)} %pad_maximum_fusion.5.sent), custom_call_target="tpu_custom_call" | custom-call | bytes 251658240 | tf_op jit(solution)/shard_map/attend_sequence/pallas_call | solution.py:617
  476.5 1.3 copy-done.7
  477.8 2.0 reshape.419
  479.8 4.2 copy.215
  484.0 2.3 slice_bitcast_fusion
  486.3 2.3 copy.210
  488.5 1.9 fusion.14
  490.5 6.9 convolution_convert_fusion.2
  497.4 80.3 %middle_sum.1 = (f32[256,2048]{1,0:T(8,128)S(1)}, bf16[8,256,2048]{2,1,0:T(8,128)(2,1)}) custom-call(bf16[8,256,2048]{2,1,0:T(8,128)(2,1)} %bitcast.205, bf16[256,2048]{1,0:T(8,128)(2,1)S(1)} %bitcast.192, f32[1,2048]{1,0:T(1,128)S(1)} %reshape.417.refs_2_), custom_call_target="tpu_custom_call" | custom-call | bytes 251658240 | tf_op jit(solution)/shard_map/middle_sum/pallas_call | solution.py:334
  579.1 17.7 %fusion.1 = f32[2048,1536]{0,1:T(8,128)S(1)} fusion(bf16[2048,2048]{1,0:T(8,128)(2,1)} %bitcast.247, bf16[2048,2304]{1,0:T(8,128)(2,1)} %all-gather.7.cloned.1.call-done), kind=kOutput, calls=%fused_computation.11 | convolution fusion | flops 12884901888 | bytes 27262976 | tf_op jit(solution)/shard_map/dot_general | solution.py:74
  596.8 4.6 copy-done.18
  601.4 2.0 multiply_convert_fusion.2
  603.4 11.2 convolution_convert_fusion.1
  614.6 81.9 %result_sum.1 = (bf16[256,2048]{1,0:T(8,128)(2,1)S(1)}, f32[256,2048]{1,0:T(8,128)S(1)}, f32[16,2048]{1,0:T(8,128)S(1)}, bf16[8,256,2048]{2,1,0:T(8,128)(2,1)}) custom-call(bf16[8,256,2048]{2,1,0:T(8,128)(2,1)} %bitcast.208, f32[256,2048]{1,0:T(8,128)} %copy-done.1, bf16[256,2048]{1,0:T(8,128)(2,1)S(1)} %bitcast.197, f32[256,1]{1,0:T(8,128)S(1)} %copy.209.refs_3_, ...), custom_call_target="tpu_custom_call" | custom-call | bytes 251658240 | tf_op jit(solution)/shard_map/result_sum/pallas_call | solution.py:334
  698.8 10.4 convolution_convert_fusion.4
  709.2 16.9 %multiply_convert_fusion.1 = (bf16[2048,768]{0,1:T(8,128)(2,1)}, bf16[2048,768]{0,1:T(8,128)(2,1)}) fusion(f32[2048,1536]{0,1:T(8,128)} %copy-done.18, bf16[2048,2048]{1,0:T(8,128)(2,1)} %bitcast.254, bf16[2048,2304]{1,0:T(8,128)(2,1)} %all-gather.7.cloned.1.call-done), kind=kOutput, calls=%fused_computation.7 | convolution fusion | flops 6462898176 | bytes 30408704 | tf_op jit(solution)/shard_map/dot_general | solution.py:74
  726.1 19.4 %convolution_convert_fusion = bf16[2048,2048]{1,0:T(8,128)(2,1)} fusion(bf16[2048,2304]{1,0:T(8,128)(2,1)} %all-gather.7.cloned.1.call-done, bf16[2048,768]{0,1:T(8,128)(2,1)} %get-tuple-element.138, bf16[2048,768]{0,1:T(8,128)(2,1)} %get-tuple-element.137), kind=kOutput, calls=%fused_computation.1 | convolution fusion | flops 12901679104 | bytes 20971520 | tf_op jit(solution)/shard_map/dot_general | solution.py:68
  745.6 82.7 %middle_back_sum.1 = (f32[256,2048]{1,0:T(8,128)S(1)}, f32[16,2048]{1,0:T(8,128)S(1)}, bf16[8,256,2048]{2,1,0:T(8,128)(2,1)}) custom-call(bf16[8,256,2048]{2,1,0:T(8,128)(2,1)} %bitcast.209, f32[256,2048]{1,0:T(8,128)S(1)} %copy-done.2, f32[1,2048]{1,0:T(1,128)S(1)} %reshape.417.refs_2_, f32[256,2048]{1,0:T(8,128)} %copy-done.10), custom_call_target="tpu_custom_call" | custom-call | bytes 251658240 | tf_op jit(solution)/shard_map/middle_back_sum/pallas_call | solution.py:334
  828.3 7.6 multiply_convert_fusion.3
  835.9 1.6 reshape.438
  837.5 1.6 copy.231.sent
  839.2 1.6 copy-done.6
  840.8 75.2 %attend_sequence_back.1 = bf16[4,512,512]{2,1,0:T(8,128)(2,1)S(1)} custom-call(bf16[4,512,256]{2,1,0:T(8,128)(2,1)S(1)} %copy.231.sent, bf16[4,512,512]{2,1,0:T(8,128)(2,1)S(1)} %copy-done.6, f32[2048,256]{1,0:T(8,128)} %copy-done.7, f32[2,1,2048]{2,1,0:T(1,128)S(1)} %get-tuple-element.39.log_total), custom_call_target="tpu_custom_call" | custom-call | bytes 314572800 | tf_op jit(solution)/shard_map/attend_sequence_back/pallas_call | solution.py:643
  918.3 1.6 convert_element_type.286
  919.8 2.1 copy.234
  921.9 2.0 copy.235
  923.9 1.9 broadcast_multiply_fusion
  926.1 1.9 copy-done.15
  930.6 1.6 copy-done.22
  933.9 2.4 convolution_convert_fusion.6
  936.5 4.7 convolution_convert_fusion.5
  941.2 1.8 pad_maximum_fusion.3
  943.1 19.4 %convolution_convert_fusion.3 = bf16[2048,1536]{1,0:T(8,128)(2,1)} fusion(bf16[2048,2048]{1,0:T(8,128)(2,1)} %bitcast.248, bf16[2048,768]{0,1:T(8,128)(2,1)} %get-tuple-element.138, bf16[2048,768]{0,1:T(8,128)(2,1)} %get-tuple-element.137), kind=kOutput, calls=%fused_computation.4 | convolution fusion | flops 12900630528 | bytes 20971520 | tf_op jit(solution)/shard_map/dot_general | solution.py:62
  963.3 19.3 %reduce-scatter.8.cloned.1.call-done = bf16[512,768]{1,0:T(8,128)(2,1)} async-done(((bf16[2048,768]{1,0:T(8,128)(2,1)}), bf16[512,768]{1,0:T(8,128)(2,1)}) %reduce-scatter.8.cloned.1.call-update) | async-done | bytes 786448 | tf_op jit(solution)/shard_map/reduce_scatter | solution.py:1122
  982.6 3.7 all-to-all-start.4
  986.2 12.3 fusion.15
  998.6 46.6 %reduce-scatter.4.cloned.1.call-done = bf16[512,768]{0,1:T(8,128)(2,1)} async-done(((bf16[2048,768]{0,1:T(8,128)(2,1)}), bf16[512,768]{0,1:T(8,128)(2,1)}) %reduce-scatter.4.cloned.1.call-update) | async-done | bytes 786448 | tf_op jit(solution)/shard_map/reduce_scatter | solution.py:1122
  1045.1 2.3 copy.221
  1047.4 4.4 all-to-all-start.2
  1051.8 12.7 add_convert_fusion
  1064.6 6.9 fusion.39
  1071.5 87.2 %reduce-scatter.6.cloned.1.call-done = bf16[512,1536]{1,0:T(8,128)(2,1)} async-done(((bf16[2048,1536]{1,0:T(8,128)(2,1)}), bf16[512,1536]{1,0:T(8,128)(2,1)}) %reduce-scatter.6.cloned.1.call-update) | async-done | bytes 1572880 | tf_op jit(solution)/shard_map/reduce_scatter | solution.py:1122
  1158.6 4.3 all-to-all-start.3
  1163.0 57.6 %inputs_back_sum.1 = (f32[256,2048]{1,0:T(8,128)S(1)}, f32[16,2048]{1,0:T(8,128)S(1)}) custom-call(bf16[8,256,2048]{2,1,0:T(8,128)(2,1)} %bitcast.206, bf16[256,2048]{1,0:T(8,128)(2,1)S(1)} %bitcast.193, f32[1,2048]{1,0:T(1,128)S(1)} %reshape.420.refs_2_, f32[256,2048]{1,0:T(8,128)S(1)} %copy-done.4), custom_call_target="tpu_custom_call" | custom-call | bytes 251658240 | tf_op jit(solution)/shard_map/inputs_back_sum/pallas_call | solution.py:334
  1222.1 7.7 dynamic_update_slice.3
  1233.1 124.9 %all-reduce.8.cloned.1.call-done = f32[37152]{0:T(1024)} async-done(((f32[37152]{0:T(1024)}), f32[37152]{0:T(1024)}) %all-reduce.8.cloned.1.call-update) | async-done | bytes 148624
  1361.4 1.4 fusion.37
  1362.8 1.4 fusion.38
  1370.3 1.7 convert_bitcast_fusion.1
  (251 shorter events, 56.7 us)
Async XLA Ops:
  8.0 9.0 copy-start.51
  8.0 9.2 copy-start.57
  8.0 9.2 copy-start.58
  8.0 9.2 copy-start.59
  8.1 9.2 copy-start.60
  10.1 20.5 %copy-start.34 = (bf16[64,6144]{1,0:T(8,128)(2,1)S(1)}, bf16[64,6144]{1,0:T(8,128)(2,1)}, u32[]{:S(2)}) copy-start(bf16[64,6144]{1,0:T(8,128)(2,1)} %param.29) | copy-start | bytes 2359300
  12.1 18.6 %copy-start.35 = (bf16[64,6144]{1,0:T(8,128)(2,1)S(1)}, bf16[64,6144]{1,0:T(8,128)(2,1)}, u32[]{:S(2)}) copy-start(bf16[64,6144]{1,0:T(8,128)(2,1)} %param.30) | copy-start | bytes 2359300
  13.1 17.7 %copy-start.36 = (bf16[6144,64]{0,1:T(8,128)(2,1)S(1)}, bf16[6144,64]{0,1:T(8,128)(2,1)}, u32[]{:S(2)}) copy-start(bf16[6144,64]{0,1:T(8,128)(2,1)} %param.31) | copy-start | bytes 2359300
  13.2 16.5 %all-to-all-start = ((bf16[8,64,768]{2,1,0:T(8,128)(2,1)}), bf16[8,64,768]{2,1,0:T(8,128)(2,1)S(1)}, u32[]{:S(2)}, u32[]{:S(2)}) async-start(bf16[8,64,768]{2,1,0:T(8,128)(2,1)} %copy.200), calls=%async_computation | async-start | bytes 1572864 | tf_op jit(solution)/shard_map/all_to_all | solution.py:1036
  17.0 312.8 %all-reduce.6.cloned.1.call-start = ((), (), s32[]{:S(2)}) async-start(), calls=%async_computation.13 | async-start | bytes 151552
  18.3 366.2 %all-gather.5.cloned.1.call-start = ((), (), s32[]{:S(2)}) async-start(), calls=%async_computation.8 | async-start | bytes 3932160 | tf_op jit(solution)/shard_map/all_gather | solution.py:1038
  30.5 548.5 %all-gather.7.cloned.1.call-start = ((), (), s32[]{:S(2)}) async-start(), calls=%async_computation.9 | async-start | bytes 11796480 | tf_op jit(solution)/shard_map/all_gather | solution.py:1038
  31.6 32.9 %copy-start = (bf16[1,256,2048]{2,1,0:T(8,128)(2,1)S(1)}, bf16[1,256,2048]{2,1,0:T(8,128)(2,1)}, u32[]{:S(2)}) copy-start(bf16[1,256,2048]{2,1,0:T(8,128)(2,1)} %param.16) | copy-start | bytes 3145732
  64.4 918.1 %reduce-scatter.8.cloned.1.call-start = ((), (), s32[]{:S(2)}) async-start(), calls=%async_computation.12 | async-start | bytes 3932160 | tf_op jit(solution)/shard_map/reduce_scatter | solution.py:1122
  68.1 2.1 copy-start.55
  68.1 2.8 copy-start.56
  333.2 41.1 %copy-start.45 = (f32[32,64]{1,0:T(8,128)}, f32[32,64]{1,0:T(8,128)S(1)}, u32[]{:S(2)}) copy-start(f32[32,64]{1,0:T(8,128)S(1)} %get-tuple-element.170) | copy-start | bytes 24580
  334.5 39.8 %copy-start.40 = (bf16[37120]{0:T(1024)(128)(2,1)S(1)}, bf16[37120]{0:T(1024)(128)(2,1)}, u32[]{:S(2)}) copy-start(bf16[37120]{0:T(1024)(128)(2,1)} %all-reduce.6.cloned.1.call-done) | copy-start | bytes 222724
  334.5 40.3 %copy-start.42 = (bf16[32,1024]{1,0:T(8,128)(2,1)S(1)}, bf16[32,1024]{1,0:T(8,128)(2,1)}, u32[]{:S(2)}) copy-start(bf16[32,1024]{1,0:T(8,128)(2,1)} %slice.169) | copy-start | bytes 196612
  374.7 19.8 %copy-start.47 = (f32[128]{0:T(128)}, f32[128]{0:T(128)S(1)}, u32[]{:S(2)}) copy-start(f32[128]{0:T(128)S(1)} %reshape.415) | copy-start | bytes 1540
  374.8 19.0 %copy-start.49 = (f32[128]{0:T(128)}, f32[128]{0:T(128)S(1)}, u32[]{:S(2)}) copy-start(f32[128]{0:T(128)S(1)} %reshape.414) | copy-start | bytes 1540
  384.5 13.5 copy-start.52
  392.2 5.8 copy-start.14
  393.5 4.5 copy-start.38
  396.8 1.3 copy-start.16
  476.5 1.4 copy-start.7
  577.7 1.3 copy-start.1
  596.8 4.6 copy-start.18
  603.4 11.3 copy-start.11
  726.1 19.4 %copy-start.2 = (f32[256,2048]{1,0:T(8,128)S(1)}, f32[256,2048]{1,0:T(8,128)}, u32[]{:S(2)}) copy-start(f32[256,2048]{1,0:T(8,128)} %copy-done.1) | copy-start | bytes 6291460
  745.6 82.8 %copy-start.31 = (f32[2048,2,128]{0,2,1:T(8,128)S(1)}, f32[2048,2,128]{0,2,1:T(8,128)}, u32[]{:S(2)}) copy-start(f32[2048,2,128]{0,2,1:T(8,128)} %copy.215) | copy-start | bytes 6291460
  745.6 82.8 %copy-start.32 = (bf16[256,2048]{1,0:T(8,128)(2,1)S(1)}, bf16[256,2048]{1,0:T(8,128)(2,1)}, u32[]{:S(2)}) copy-start(bf16[256,2048]{1,0:T(8,128)(2,1)} %copy.210) | copy-start | bytes 3145732
  745.6 82.8 %copy-start.44 = (f32[2048,2]{0,1:T(2,128)S(1)}, f32[2048,2]{0,1:T(2,128)}, u32[]{:S(2)}) copy-start(f32[2048,2]{0,1:T(2,128)} %copy-done.43) | copy-start | bytes 49156
  828.3 7.6 copy-start.3
  839.2 1.6 copy-start.6
  917.1 128.0 %reduce-scatter.4.cloned.1.call-start = ((), (), s32[]{:S(2)}) async-start(), calls=%async_computation.10 | async-start | bytes 3932160 | tf_op jit(solution)/shard_map/reduce_scatter | solution.py:1122
  918.3 5.7 copy-start.20
  923.9 2.1 copy-start.17
  923.9 2.1 copy-start.39
  925.8 2.2 copy-start.15
  925.8 2.2 copy-start.50
  928.9 1.4 copy-start.27
  928.9 4.7 slice-start.2
  930.4 6.0 copy-start.33
  930.4 1.8 copy-start.22
  930.4 1.8 copy-start.48
  930.4 3.3 slice-start.3
  932.2 1.7 copy-start.61
  932.2 4.1 slice-start
  933.9 2.5 slice-start.1
  933.9 2.5 copy-start.37
  943.1 215.5 %reduce-scatter.6.cloned.1.call-start = ((), (), s32[]{:S(2)}) async-start(), calls=%async_computation.11 | async-start | bytes 7864320 | tf_op jit(solution)/shard_map/reduce_scatter | solution.py:1122
  982.6 64.8 %all-to-all-start.4 = ((bf16[8,64,768]{2,1,0:T(8,128)(2,1)}), bf16[8,64,768]{2,1,0:T(8,128)(2,1)S(1)}, u32[]{:S(2)}, u32[]{:S(2)}) async-start(bf16[8,64,768]{2,1,0:T(8,128)(2,1)} %bitcast.230), calls=%async_computation.7 | async-start | bytes 1572864 | tf_op jit(solution)/shard_map/all_to_all | solution.py:1123
  998.5 53.3 %copy-start.25 = (bf16[2048,16]{1,0:T(8,128)(2,1)S(1)}, bf16[2048,16]{1,0:T(8,128)(2,1)}, u32[]{:S(2)}) copy-start(bf16[2048,16]{1,0:T(8,128)(2,1)} %copy-done.24) | copy-start | bytes 196612
  1047.4 17.2 %copy-start.29 = (bf16[8,64,768]{2,1,0:T(8,128)(2,1)}, bf16[8,64,768]{2,1,0:T(8,128)(2,1)S(1)}, u32[]{:S(2)}) copy-start(bf16[8,64,768]{2,1,0:T(8,128)(2,1)S(1)} %all-to-all-done.4) | copy-start | bytes 2359300
  1047.4 24.1 %all-to-all-start.2 = ((bf16[8,64,768]{2,1,0:T(8,128)(2,1)}), bf16[8,64,768]{2,1,0:T(8,128)(2,1)}, u32[]{:S(2)}, u32[]{:S(2)}) async-start(bf16[8,64,768]{2,1,0:T(8,128)(2,1)} %bitcast.60), calls=%async_computation.3 | async-start | bytes 1572864 | tf_op jit(solution)/shard_map/all_to_all | solution.py:1123
  1071.4 91.5 %copy-start.4 = (f32[256,2048]{1,0:T(8,128)S(1)}, f32[256,2048]{1,0:T(8,128)}, u32[]{:S(2)}) copy-start(f32[256,2048]{1,0:T(8,128)} %copy-done.3) | copy-start | bytes 6291460
  1158.6 211.7 %all-to-all-start.3 = ((bf16[8,64,1536]{2,1,0:T(8,128)(2,1)}), bf16[8,64,1536]{2,1,0:T(8,128)(2,1)}, u32[]{:S(2)}, u32[]{:S(2)}) async-start(bf16[8,64,1536]{2,1,0:T(8,128)(2,1)} %bitcast.220), calls=%async_computation.5 | async-start | bytes 3145728 | tf_op jit(solution)/shard_map/all_to_all | solution.py:1123
  1162.9 195.1 %all-reduce.8.cloned.1.call-start = ((), (), s32[]{:S(2)}) async-start(), calls=%async_computation.14 | async-start | bytes 303104
  1220.6 1.3 copy-start.8
  1221.9 8.7 copy-start.54
  1222.0 142.1 %copy-start.30 = (bf16[8,64,768]{2,1,0:T(8,128)(2,1)S(1)}, bf16[8,64,768]{2,1,0:T(8,128)(2,1)}, u32[]{:S(2)}) copy-start(bf16[8,64,768]{2,1,0:T(8,128)(2,1)} %copy-done.29) | copy-start | bytes 2359300
  1372.0 2.6 copy-start.13
  1373.3 2.2 copy-start.9
  (13 other events, 12.5 us)
Sparse Core Ops, SparseCore 0:
  24.0 305.7 all-reduce.5
  1233.2 124.7 all-reduce.7
Sparse Core Ops, SparseCore 1:
  30.6 60.6 all-gather.4
  92.7 165.2 all-gather.6
  917.2 65.3 reduce-scatter.7
  984.9 60.2 reduce-scatter.3
  1047.4 111.1 reduce-scatter.5
